TPU v7x, 512 devices: a whole 4x8x8 slice. The times are simulated.
512 devices in a mesh: space: 128 (over x, y, z_hi, core), modes: 4 (over z_lo).
Axes of the slice: x: 4, y: 8, z: 8 (z_hi: 2, z_lo: 4; z = z_hi * 4 + z_lo), core: 2. Of those that a mesh axis runs over, the one named last changes fastest.
Arguments:
- voltage_expansion: float32 [220, 128, 2048], P('modes', 'space'), may hold values from -6 to 6
- current_injection: float32 [220, 128, 2048], P('modes', 'space'), may hold values from -48 to 48
- thermal_state: float32 [220, 128, 2048], P('modes', 'space'), may hold values from -6 to 6
- average_electric_transport: float32 [128, 2048], P('space'), may hold values from 0.5 to 4
- material_zone: int32 [128, 2048], P('space'), may hold values from 0 to 3
- zone_relative_response: float32 [4, 9], replicated, may hold values from 0.02 to 0.12
- polynomial_exponent_rows: int32 [220, 9], replicated, may hold values from 0 to 3, as said below
- quadrature_abscissa_choice: int32 [512, 9], replicated, may hold values from 0 to 4
- quadrature_integer_share: int32 [512], replicated, may hold values from 1 to 1024
Outputs:
- relaxed_voltage: float32 [220, 128, 2048], P('modes', 'space')
- advanced_thermal_state: float32 [220, 128, 2048], P('modes', 'space')
Inputs may be any that keep to these rules, and one draw needn't show every extreme that they name: `polynomial_exponent_rows`: the rows are the 220 multi-indices of total degree at most 3 over 9 parameters, each once.
All inputs are finite; a program needn't handle non-finite values.
Results may differ from a plain program's by a relative error of at most 0.0003.
Values sent between devices are 32-bit elements; how exact they have to be, the bound alone decides.
A program may use at most 64 MiB of HBM per device.

v0:
```python
import jax
import jax.numpy as jnp
from jax import lax
from jax.sharding import PartitionSpec as P

NY = 256
NZ = 8


HERMITE_NODES = (
    0.0,
    1.355626179974266,
    -1.355626179974266,
    2.8569700138728056,
    -2.8569700138728056,
)


def padded_2(block, sides, width):
    for axis, dim in sides:
        count = lax.axis_size(axis)
        forward = [(i, i + 1) for i in range(count - 1)]
        backward = [(target, source) for source, target in forward]
        low = lax.ppermute(
            lax.slice_in_dim(block, block.shape[dim] - width, None, axis=dim), axis, forward
        )
        high = lax.ppermute(lax.slice_in_dim(block, 0, width, axis=dim), axis, backward)
        block = jnp.concatenate([low, block, high], axis=dim)
    return block


def neighbours(field):
    column_ids = jnp.arange(field.shape[-1])
    depth_pos = column_ids % NZ
    row_pos = column_ids // NZ
    z_next = jnp.where(depth_pos < NZ - 1, jnp.roll(field, -1, -1), 0.0)
    z_prev = jnp.where(depth_pos > 0, jnp.roll(field, 1, -1), 0.0)
    y_next = jnp.where(row_pos < NY - 1, jnp.roll(field, -NZ, -1), 0.0)
    y_prev = jnp.where(row_pos > 0, jnp.roll(field, NZ, -1), 0.0)
    return (z_next, z_prev, y_next, y_prev)


def diffusion_operator_weights(padded):
    center = padded[..., 1:-1, :]
    z_next, z_prev, y_next, y_prev = neighbours(center)
    return (
        6.0 * center - padded[..., 2:, :] - padded[..., :-2, :] - z_next - z_prev - y_next - y_prev
    )


def gradient(padded):
    center = padded[..., 1:-1, :]
    z_next, z_prev, y_next, y_prev = neighbours(center)
    along_x = (padded[..., 2:, :] - padded[..., :-2, :]) * 0.5
    along_y = (y_next - y_prev) * 0.5
    along_z = (z_next - z_prev) * 0.5
    return jnp.stack([along_x, along_y, along_z])


def coupling(row_table, col_table):
    offsets = row_table[:, None, :] - col_table[None, :, :]
    differ_count = jnp.sum((offsets != 0).astype(jnp.int32), axis=2)
    layers = [jnp.where(differ_count == 0, 1.0, 0.0).astype(jnp.float32)]
    for which_param in range(row_table.shape[1]):
        larger = jnp.maximum(
            row_table[:, None, which_param], col_table[None, :, which_param]
        ).astype(jnp.float32)
        linked = (jnp.abs(offsets[:, :, which_param]) == 1) & (differ_count == 1)
        layers.append(jnp.where(linked, jnp.sqrt(larger), 0.0))
    return jnp.stack(layers)


def node_values(quadrature_abscissa_choice):
    node_vals = jnp.zeros(quadrature_abscissa_choice.shape, jnp.float32)
    for which_node in range(5):
        node_vals = node_vals + jnp.where(
            quadrature_abscissa_choice == which_node, HERMITE_NODES[which_node], 0.0
        )
    return node_vals


def basis_values(polynomial_exponent_rows, node_vals):
    poly_terms = [
        jnp.ones_like(node_vals),
        node_vals,
        (node_vals * node_vals - 1.0) / jnp.sqrt(2.0),
        (node_vals * node_vals * node_vals - 3.0 * node_vals) / jnp.sqrt(6.0),
    ]
    basis_vals = jnp.ones((node_vals.shape[0], polynomial_exponent_rows.shape[0]), jnp.float32)
    for which_param in range(polynomial_exponent_rows.shape[1]):
        degree = polynomial_exponent_rows[:, which_param]
        factor = jnp.zeros_like(basis_vals)
        for which_deg in range(4):
            factor = factor + jnp.where(
                degree[None, :] == which_deg, poly_terms[which_deg][:, which_param][:, None], 0.0
            )
        basis_vals = basis_vals * factor
    return basis_vals


def on_device(
    voltage_expansion,
    current_injection,
    thermal_state,
    average_electric_transport,
    material_zone,
    zone_relative_response,
    polynomial_exponent_rows,
    quadrature_abscissa_choice,
    quadrature_integer_share,
):
    hp = lax.Precision.HIGHEST
    modes_here = voltage_expansion.shape[0]
    planes = voltage_expansion.shape[1]
    columns = voltage_expansion.shape[2]
    cell_count = planes * columns
    nreg = zone_relative_response.shape[0]
    all_modes = polynomial_exponent_rows.shape[0]
    num_points = quadrature_integer_share.shape[0]
    first_mode = lax.axis_index("modes") * modes_here
    own_table = lax.dynamic_slice_in_dim(polynomial_exponent_rows, first_mode, modes_here, 0)
    bordered_quantities = padded_2(
        jnp.stack([voltage_expansion, thermal_state]), (("space", 2),), 1
    )
    pot_padded = bordered_quantities[0]
    thermal_state_bordered = bordered_quantities[1]
    sens_cell = jnp.zeros((zone_relative_response.shape[1],) + material_zone.shape, jnp.float32)
    for which_region in range(nreg):
        sens_cell = sens_cell + jnp.where(
            material_zone[None] == which_region,
            zone_relative_response[which_region][:, None, None],
            0.0,
        )
    coeff = (
        jnp.concatenate([jnp.ones((1,) + material_zone.shape, jnp.float32), sens_cell])
        * average_electric_transport
    )
    coeff_flat = coeff.reshape(coeff.shape[0], cell_count)
    flat_rough = diffusion_operator_weights(pot_padded).reshape(modes_here, cell_count)
    row_coup = coupling(own_table, polynomial_exponent_rows)
    mixed = jnp.einsum(
        "mij,jc->mic",
        row_coup,
        lax.all_gather(flat_rough, "modes", axis=0, tiled=True),
        precision=hp,
    )
    applied = jnp.sum(coeff_flat[:, None, :] * mixed, axis=0)
    applied = applied.reshape(modes_here, planes, columns)
    relaxed_voltage = voltage_expansion + 0.8 * (current_injection - applied) / (
        6.0 * average_electric_transport
    )
    node_vals = node_values(quadrature_abscissa_choice)
    basis_vals = basis_values(polynomial_exponent_rows, node_vals)
    new_padded = padded_2(relaxed_voltage, (("space", 1),), 1)
    grads = gradient(new_padded)
    point_grads = jnp.einsum(
        "qi,kixn->kqxn",
        basis_vals,
        lax.all_to_all(grads, "modes", split_axis=3, concat_axis=1, tiled=True),
        precision=hp,
    )
    quarter = columns // lax.axis_size("modes")
    offset = lax.axis_index("modes") * quarter
    cond_part = lax.dynamic_slice_in_dim(average_electric_transport, offset, quarter, 1)
    region_part = lax.dynamic_slice_in_dim(material_zone, offset, quarter, 1)
    cond_lift = 1.0 + jnp.dot(zone_relative_response, node_vals.T, precision=hp)
    spread = jnp.zeros((num_points, planes, quarter), jnp.float32)
    for which_region in range(nreg):
        spread = spread + jnp.where(
            region_part[None] == which_region, cond_lift[which_region][:, None, None], 0.0
        )
    joule_heat = cond_part * spread * jnp.sum(point_grads * point_grads, axis=0)
    weighted = (
        basis_vals.T
        * quadrature_integer_share[None, :].astype(jnp.float32)
        / (512.0 * num_points * all_modes)
    )
    heat_points = jnp.einsum("iq,qxn->ixn", weighted, joule_heat, precision=hp)
    thermal_expansion_terms = lax.all_to_all(
        heat_points, "modes", split_axis=0, concat_axis=2, tiled=True
    )
    advanced_thermal_state = thermal_state + 0.1 * (
        thermal_expansion_terms - 1.5 * diffusion_operator_weights(thermal_state_bordered)
    )
    return (relaxed_voltage, advanced_thermal_state)


def solution(mesh):
    in_specs = (
        P("modes", "space", None),
        P("modes", "space", None),
        P("modes", "space", None),
        P("space", None),
        P("space", None),
        P(),
        P(),
        P(),
        P(),
    )
    out_specs = (P("modes", "space", None), P("modes", "space", None))
    return jax.shard_map(
        on_device, mesh=mesh, in_specs=in_specs, out_specs=out_specs, check_vma=False
    )
```

profile of v0, /device:TPU:61, one launch (start us, length us, event | category | flops | bytes accessed | tf_op | source)
XLA Modules:
  0.0 265.5 jit_solution(5457627602112726379)
XLA Ops:
  7.2 1.4 copy_bitcast_fusion
  9.5 2.6 collective-permute-start.1
  12.1 10.5 %collective-permute-start = (f32[2,55,1,2048]{3,0,2,1:T(2,128)S(1)}, f32[2,55,1,2048]{3,0,2,1:T(2,128)}, u32[]{:S(2)}, u32[]{:S(2)}) collective-permute-start(f32[2,55,1,2048]{3,0,2,1:T(2,128)S(1)} %copy.62), channel_id=1, source_target_pairs={{0,4},{4,8},{8,12},{12,16},{16,20},{20,24},{24,28},{28,32},{32,36}... | collective-permute-start | bytes 2703368 | tf_op jit(solution)/shard_map/ppermute | solution.py:24
  27.4 27.7 %collective-permute-done.1 = f32[2,55,1,2048]{3,0,2,1:T(2,128)} collective-permute-done((f32[2,55,1,2048]{3,0,2,1:T(2,128)S(1)}, f32[2,55,1,2048]{3,0,2,1:T(2,128)}, u32[]{:S(2)}, u32[]{:S(2)}) %collective-permute-start.1) | collective-permute-done | bytes 901152 | tf_op jit(solution)/shard_map/ppermute | solution.py:27
  55.0 1.7 copy.65
  56.7 8.6 %collective-permute-done = f32[2,55,1,2048]{3,0,2,1:T(2,128)} collective-permute-done((f32[2,55,1,2048]{3,0,2,1:T(2,128)S(1)}, f32[2,55,1,2048]{3,0,2,1:T(2,128)}, u32[]{:S(2)}, u32[]{:S(2)}) %collective-permute-start) | collective-permute-done | bytes 901152 | tf_op jit(solution)/shard_map/ppermute | solution.py:24
  65.4 1.7 copy.64
  74.1 42.7 %all-gather.3.cloned.1.call-done = f32[220,1,2048]{2,1,0:T(1,128)} async-done(((f32[55,1,2048]{2,1,0:T(1,128)}), f32[220,1,2048]{2,1,0:T(1,128)}) %all-gather.3.cloned.1.call-update) | async-done | bytes 1802256 | tf_op jit(solution)/shard_map/all_gather | solution.py:144
  116.8 5.9 %multiply_reduce_fusion = f32[55,2048]{1,0:T(8,128)S(1)} fusion(f32[10,55,220]{2,1,0:T(8,128)} %select_dynamic-update-slice_fusion, f32[10,2048]{1,0:T(8,128)S(1)} %multiply_bitcast_fusion.1, f32[220,1,2048]{2,1,0:T(1,128)} %all-gather.3.cloned.1.call-done), kind=kOutput, calls=%fused_computation | convolution fusion | flops 2975836160 | bytes 2818720 | tf_op jit(solution)/shard_map/mij,jc->mic/dot_general | solution.py:141
  123.6 3.1 %collective-permute-start.2 = (f32[55,1,2048]{2,0,1:T(8,128)S(1)}, f32[55,1,2048]{2,0,1:T(8,128)S(1)}, u32[]{:S(2)}, u32[]{:S(2)}) collective-permute-start(f32[55,1,2048]{2,0,1:T(8,128)S(1)} %fusion.40), channel_id=1, source_target_pairs={{4,0},{8,4},{12,8},{16,12},{20,16},{24,20},{28,24},{32,28},{36,32}... | collective-permute-start | bytes 1351688 | tf_op jit(solution)/shard_map/ppermute | solution.py:27
  126.7 6.6 %collective-permute-start.3 = (f32[55,1,2048]{2,0,1:T(8,128)S(1)}, f32[55,1,2048]{2,0,1:T(8,128)S(1)}, u32[]{:S(2)}, u32[]{:S(2)}) collective-permute-start(f32[55,1,2048]{2,0,1:T(8,128)S(1)} %fusion.40), channel_id=1, source_target_pairs={{0,4},{4,8},{8,12},{12,16},{16,20},{20,24},{24,28},{28,32},{32,36}... | collective-permute-start | bytes 1351688 | tf_op jit(solution)/shard_map/ppermute | solution.py:24
  133.7 9.7 %collective-permute-done.2 = f32[55,1,2048]{2,0,1:T(8,128)S(1)} collective-permute-done((f32[55,1,2048]{2,0,1:T(8,128)S(1)}, f32[55,1,2048]{2,0,1:T(8,128)S(1)}, u32[]{:S(2)}, u32[]{:S(2)}) %collective-permute-start.2) | collective-permute-done | bytes 450592 | tf_op jit(solution)/shard_map/ppermute | solution.py:27
  143.4 11.2 %collective-permute-done.3 = f32[55,1,2048]{2,0,1:T(8,128)S(1)} collective-permute-done((f32[55,1,2048]{2,0,1:T(8,128)S(1)}, f32[55,1,2048]{2,0,1:T(8,128)S(1)}, u32[]{:S(2)}, u32[]{:S(2)}) %collective-permute-start.3) | collective-permute-done | bytes 450592 | tf_op jit(solution)/shard_map/ppermute | solution.py:24
  154.8 3.1 %copy.71 = f32[3,55,1,2048]{1,0,2,3:T(4,128)} copy(f32[3,55,1,2048]{3,1,2,0:T(8,128)S(1)} %pad_maximum_fusion.1) | data formatting | bytes 2703360 | tf_op jit(solution)/shard_map/stack | solution.py:57
  157.9 6.6 %reshape.2106 = f32[4,1,84480]{2,1,0:T(1,128)} reshape(f32[2048,1,3,55]{3,2,1,0:T(4,128)} %bitcast.196) | data formatting | bytes 2703360
  164.5 3.7 %all-to-all-start = ((f32[4,1,84480]{2,1,0:T(1,128)}), f32[4,1,84480]{2,1,0:T(1,128)S(1)}, u32[]{:S(2)}, u32[]{:S(2)}) async-start(f32[4,1,84480]{2,1,0:T(1,128)} %reshape.2106), calls=%async_computation | async-start | bytes 2703360 | tf_op jit(solution)/shard_map/all_to_all | solution.py:159
  169.7 29.9 %all-to-all-done = f32[4,1,84480]{2,1,0:T(1,128)S(1)} async-done(((f32[4,1,84480]{2,1,0:T(1,128)}), f32[4,1,84480]{2,1,0:T(1,128)S(1)}, u32[]{:S(2)}, u32[]{:S(2)}) %all-to-all-start) | async-done | bytes 1351712 | tf_op jit(solution)/shard_map/all_to_all | solution.py:159
  200.1 5.6 %reduce.20 = f32[4,84480]{1,0:T(4,128)} reduce(f32[4,1,84480]{2,1,0:T(1,128)S(1)} %all-to-all-done, f32[]{:T(128)} %broadcast.1558), dimensions={1}, to_apply=%all_to_all.24.reduce_sub_computation | reduce | bytes 2703364 | tf_op jit(solution)/shard_map/all_to_all | solution.py:159
  205.7 6.9 %reshape.2107 = f32[2048,1,3,55]{3,2,1,0:T(4,128)} reshape(f32[4,84480]{1,0:T(4,128)} %reduce.20) | data formatting | bytes 2703360
  212.6 4.6 %copy.79 = f32[3,55,1,4,512]{4,3,1,0,2:T(4,128)} copy(f32[3,55,1,4,512]{1,0,4,3,2:T(4,128)} %bitcast.197) | data formatting | bytes 2703360 | tf_op jit(solution)/shard_map/all_to_all | solution.py:159
  217.2 1.8 copy.73
  219.0 1.3 reshape.2092
  220.3 6.3 %multiply_reduce_fusion.1 = f32[512,512]{1,0:T(8,128)S(1)} fusion(f32[3,220,512]{2,1,0:T(8,128)} %reshape.2092, f32[512]{0:T(512)S(1)} %bitcast.231, f32[512]{0:T(512)S(1)} %bitcast.279, f32[512]{0:T(512)S(1)} %bitcast.259, f32[220]{0:T(256)S(1)} %get-tuple-element.133, f32[512]{0:T(512)S(1)} %bitcast.233, f32[512]{0:T(512)S(1)} %bitcast.277, ...), kind=kOutput, calls=%fused_computation.1 | convolution fusion | flops 2084474880 | bytes 2469412 | tf_op jit(solution)/shard_map/qi,kixn->kqxn/dot_general | solution.py:156
  226.6 3.1 %convolution_bitcast_fusion = f32[220,1,512]{2,0,1:T(8,128)S(1)} fusion(f32[512,512]{1,0:T(8,128)S(1)} %multiply_reduce_fusion.1, f32[512]{0:T(512)S(1)} %bitcast.285, f32[512]{0:T(512)S(1)} %bitcast.286, f32[512]{0:T(512)S(1)} %bitcast.287, f32[512]{0:T(512)S(1)} %bitcast.284, f32[512]{0:T(512)S(1)} %bitcast.283, pred[512]{0:T(512)(128)(4,1)S(1)} %copy-done.13, ...), kind=kOutput, calls=%fused_computation.8 | convolution fusion | flops 701628416 | bytes 1582628 | tf_op jit(solution)/shard_map/iq,qxn->ixn/dot_general | solution.py:178
  230.9 3.7 %all-to-all-start.1 = ((f32[220,1,512]{2,1,0:T(1,128)}), f32[220,1,512]{2,1,0:T(1,128)S(1)}, u32[]{:S(2)}, u32[]{:S(2)}) async-start(f32[220,1,512]{2,1,0:T(1,128)} %copy.74), calls=%async_computation.1 | async-start | bytes 901120 | tf_op jit(solution)/shard_map/all_to_all | solution.py:179
  234.9 1.2 copy.77
  236.2 11.5 %all-to-all-done.1 = f32[220,1,512]{2,1,0:T(1,128)S(1)} async-done(((f32[220,1,512]{2,1,0:T(1,128)}), f32[220,1,512]{2,1,0:T(1,128)S(1)}, u32[]{:S(2)}, u32[]{:S(2)}) %all-to-all-start.1) | async-done | bytes 450592 | tf_op jit(solution)/shard_map/all_to_all | solution.py:179
  247.7 1.9 reduce.11
  249.6 1.9 all_to_all.28
  251.5 2.1 copy.75
  253.6 2.1 all_to_all.30
  255.7 1.7 fusion.28
  (101 shorter events, 18.6 us)
Async XLA Ops:
  7.2 109.6 %all-gather.3.cloned.1.call-start = ((), (), s32[]{:S(2)}) async-start(), calls=%async_computation.2 | async-start | bytes 2252800 | tf_op jit(solution)/shard_map/all_gather | solution.py:144
  8.7 14.0 %copy-start.4 = (s32[220,9]{0,1:T(8,128)S(1)}, s32[220,9]{0,1:T(8,128)}, u32[]{:S(2)}) copy-start(s32[220,9]{0,1:T(8,128)} %param.15) | copy-start | bytes 23764
  8.7 14.9 %copy-start.7 = (s32[1,2048]{1,0:T(1,128)S(1)}, s32[1,2048]{1,0:T(1,128)}, u32[]{:S(2)}) copy-start(s32[1,2048]{1,0:T(1,128)} %param.13) | copy-start | bytes 24580
  8.8 15.6 %copy-start.5 = (f32[1,2048]{1,0:T(1,128)S(1)}, f32[1,2048]{1,0:T(1,128)}, u32[]{:S(2)}) copy-start(f32[1,2048]{1,0:T(1,128)} %param.12) | copy-start | bytes 24580
  8.8 15.6 %copy-start.8 = (s32[512]{0:T(512)S(1)}, s32[512]{0:T(512)}, u32[]{:S(2)}) copy-start(s32[512]{0:T(512)} %param.17) | copy-start | bytes 6148
  8.8 16.4 %copy-start.9 = (f32[4,9]{1,0:T(4,128)S(1)}, f32[4,9]{1,0:T(4,128)}, u32[]{:S(2)}) copy-start(f32[4,9]{1,0:T(4,128)} %param.14) | copy-start | bytes 436
  9.5 45.6 %collective-permute-start.1 = (f32[2,55,1,2048]{3,0,2,1:T(2,128)S(1)}, f32[2,55,1,2048]{3,0,2,1:T(2,128)}, u32[]{:S(2)}, u32[]{:S(2)}) collective-permute-start(f32[2,55,1,2048]{3,0,2,1:T(2,128)S(1)} %copy.62), channel_id=1, source_target_pairs={{4,0},{8,4},{12,8},{16,12},{20,16},{24,20},{28,24},{32,28},{36,32}... | collective-permute-start | bytes 2703368 | tf_op jit(solution)/shard_map/ppermute | solution.py:27
  12.1 53.3 %collective-permute-start = (f32[2,55,1,2048]{3,0,2,1:T(2,128)S(1)}, f32[2,55,1,2048]{3,0,2,1:T(2,128)}, u32[]{:S(2)}, u32[]{:S(2)}) collective-permute-start(f32[2,55,1,2048]{3,0,2,1:T(2,128)S(1)} %copy.62), channel_id=1, source_target_pairs={{0,4},{4,8},{8,12},{12,16},{16,20},{20,24},{24,28},{28,32},{32,36}... | collective-permute-start | bytes 2703368 | tf_op jit(solution)/shard_map/ppermute | solution.py:24
  74.1 48.7 %copy-start.2 = (f32[55,1,2048]{2,1,0:T(1,128)S(1)}, f32[55,1,2048]{2,1,0:T(1,128)}, u32[]{:S(2)}) copy-start(f32[55,1,2048]{2,1,0:T(1,128)} %param.9) | copy-start | bytes 1351684
  74.1 48.7 %copy-start.3 = (f32[55,1,2048]{2,1,0:T(1,128)S(1)}, f32[55,1,2048]{2,1,0:T(1,128)}, u32[]{:S(2)}) copy-start(f32[55,1,2048]{2,1,0:T(1,128)} %param.10) | copy-start | bytes 1351684
  123.6 19.7 %collective-permute-start.2 = (f32[55,1,2048]{2,0,1:T(8,128)S(1)}, f32[55,1,2048]{2,0,1:T(8,128)S(1)}, u32[]{:S(2)}, u32[]{:S(2)}) collective-permute-start(f32[55,1,2048]{2,0,1:T(8,128)S(1)} %fusion.40), channel_id=1, source_target_pairs={{4,0},{8,4},{12,8},{16,12},{20,16},{24,20},{28,24},{32,28},{36,32}... | collective-permute-start | bytes 1351688 | tf_op jit(solution)/shard_map/ppermute | solution.py:27
  126.7 27.9 %collective-permute-start.3 = (f32[55,1,2048]{2,0,1:T(8,128)S(1)}, f32[55,1,2048]{2,0,1:T(8,128)S(1)}, u32[]{:S(2)}, u32[]{:S(2)}) collective-permute-start(f32[55,1,2048]{2,0,1:T(8,128)S(1)} %fusion.40), channel_id=1, source_target_pairs={{0,4},{4,8},{8,12},{12,16},{16,20},{20,24},{24,28},{28,32},{32,36}... | collective-permute-start | bytes 1351688 | tf_op jit(solution)/shard_map/ppermute | solution.py:24
  164.5 3.7 %copy-start.6 = (s32[512,9]{0,1:T(8,128)S(1)}, s32[512,9]{0,1:T(8,128)}, u32[]{:S(2)}) copy-start(s32[512,9]{0,1:T(8,128)} %param.16) | copy-start | bytes 55300
  164.5 35.0 %all-to-all-start = ((f32[4,1,84480]{2,1,0:T(1,128)}), f32[4,1,84480]{2,1,0:T(1,128)S(1)}, u32[]{:S(2)}, u32[]{:S(2)}) async-start(f32[4,1,84480]{2,1,0:T(1,128)} %reshape.2106), calls=%async_computation | async-start | bytes 2703360 | tf_op jit(solution)/shard_map/all_to_all | solution.py:159
  220.2 6.3 %copy-start.10 = (pred[512]{0:T(512)(128)(4,1)S(1)}, pred[512]{0:T(512)(128)(4,1)}, u32[]{:S(2)}) copy-start(pred[512]{0:T(512)(128)(4,1)} %get-tuple-element.12) | copy-start | bytes 1540
  220.2 6.3 %copy-start.11 = (pred[512]{0:T(512)(128)(4,1)S(1)}, pred[512]{0:T(512)(128)(4,1)}, u32[]{:S(2)}) copy-start(pred[512]{0:T(512)(128)(4,1)} %get-tuple-element.13) | copy-start | bytes 1540
  220.2 6.3 %copy-start.12 = (pred[512]{0:T(512)(128)(4,1)S(1)}, pred[512]{0:T(512)(128)(4,1)}, u32[]{:S(2)}) copy-start(pred[512]{0:T(512)(128)(4,1)} %get-tuple-element.14) | copy-start | bytes 1540
  220.2 6.3 %copy-start.13 = (pred[512]{0:T(512)(128)(4,1)S(1)}, pred[512]{0:T(512)(128)(4,1)}, u32[]{:S(2)}) copy-start(pred[512]{0:T(512)(128)(4,1)} %get-tuple-element.15) | copy-start | bytes 1540
  220.2 6.3 %copy-start.14 = (pred[220]{0:T(512)(128)(4,1)S(1)}, pred[220]{0:T(512)(128)(4,1)}, u32[]{:S(2)}) copy-start(pred[220]{0:T(512)(128)(4,1)} %get-tuple-element.106) | copy-start | bytes 664
  220.3 6.3 %copy-start.15 = (pred[220]{0:T(512)(128)(4,1)S(1)}, pred[220]{0:T(512)(128)(4,1)}, u32[]{:S(2)}) copy-start(pred[220]{0:T(512)(128)(4,1)} %get-tuple-element.107) | copy-start | bytes 664
  220.3 6.3 %copy-start.16 = (pred[220]{0:T(512)(128)(4,1)S(1)}, pred[220]{0:T(512)(128)(4,1)}, u32[]{:S(2)}) copy-start(pred[220]{0:T(512)(128)(4,1)} %get-tuple-element.108) | copy-start | bytes 664
  230.9 16.8 %all-to-all-start.1 = ((f32[220,1,512]{2,1,0:T(1,128)}), f32[220,1,512]{2,1,0:T(1,128)S(1)}, u32[]{:S(2)}, u32[]{:S(2)}) async-start(f32[220,1,512]{2,1,0:T(1,128)} %copy.74), calls=%async_computation.1 | async-start | bytes 901120 | tf_op jit(solution)/shard_map/all_to_all | solution.py:179
  249.6 6.1 %copy-start = (f32[55,1,2047]{2,0,1:T(8,128)S(1)}, f32[55,1,2047]{2,0,1:T(8,128)}, u32[]{:S(2)}) copy-start(f32[55,1,2047]{2,0,1:T(8,128)} %get-tuple-element.30) | copy-start | bytes 1351024
  249.6 6.1 %copy-start.1 = (f32[55,1,2047]{2,0,1:T(8,128)S(1)}, f32[55,1,2047]{2,0,1:T(8,128)}, u32[]{:S(2)}) copy-start(f32[55,1,2047]{2,0,1:T(8,128)} %get-tuple-element.31) | copy-start | bytes 1351024
Sparse Core Ops, SparseCore 0:
  69.9 46.8 all-gather.2
where the time goes:
time: 266 us; the launch traced here: 265 us
  waiting for transfers between devices  141 us (53%)
  local copies, waits for them, and re-layouts  44.4 us (17%)
  starting transfers between devices  30.2 us (11%)
  other arithmetic  19.7 us (7%)
  matrix products  15.4 us (6%)
  between operations  14.5 us (5%)
    all_gather x1, waiting for transfers between devices, on_device(): lax.all_gather(flat_rough, 'modes', axis=0, tiled=True)  42.7 us
    ppermute x2, waiting for transfers between devices, padded_2(): lax.ppermute(lax.slice_in_dim(block, 0, width, axis=dim), axis, backward)  37.3 us
    all_to_all x1, waiting for transfers between devices, on_device(): lax.all_to_all(grads, 'modes', split_axis=3, concat_axis=1, tiled=True)  29.9 us
    ppermute x2, waiting for transfers between devices, padded_2(): lax.ppermute(lax.slice_in_dim(block, block.shape[dim] - width, None, axis...  19.9 us
    unnamed x39, local copies, waits for them, and re-layouts  17.5 us
    ppermute x2, starting transfers between devices, padded_2(): lax.ppermute(lax.slice_in_dim(block, block.shape[dim] - width, None, axis...  17.1 us
    all_to_all x1, waiting for transfers between devices, on_device(): lax.all_to_all(heat_points, 'modes', split_axis=0, concat_axis=2, tiled=T...  11.5 us
    all_to_all x3, local copies, waits for them, and re-layouts, on_device(): lax.all_to_all(grads, 'modes', split_axis=3, concat_axis=1, tiled=True)  6.9 us
  transfers between devices with their start and end apart: 7, of which 7 were waited for; matrix products, arithmetic and copies ran while one was open for 5% of the time, Pallas kernels for 0%

commit v1 on v0

v1 whole, which is shorter than its diff:
```python
import functools
import math

import jax
import jax.numpy as jnp
from jax import lax
from jax.experimental import pallas as pl
from jax.experimental.pallas import tpu as pltpu
from jax.sharding import PartitionSpec as P

MESH = pl.DeviceIdType.MESH
F32 = jnp.float32
BF16 = jnp.bfloat16
NODE_A = 1.355626179974266
NODE_B = 2.8569700138728056
NMODE = 220
NPAR = 9
NQ = 512
NREG = 4
GRP = 55
SLOT = 56
ROWS = 4 * SLOT
KP = 256
MIX = 0.8 / 6.0
COLUMNS = 32
FAR = 100.0


def split(x):
    hi = x.astype(BF16)
    return hi, (x - hi.astype(F32)).astype(BF16)


def kernel(
    v_ref, i_ref, t_ref, avg_ref, zone_ref, zrr_ref, e_ref, n_ref, share_ref,
    rel_out, adv_out,
    sv, su, st, tfix, vc, uc, tc, rel, adv, rough, hxv, hyv, hxr, hyr, hxt, pkv, pkr, ro, ao,
    tmp, ecol, erow, hrow, ncol, basis_t, acat, bcat, wcat, rcat, pmix, gcat, jsum, jcat, lift,
    a_send, a_recv, h_send, h_recv,
):
    s = lax.axis_index("space")
    m = lax.axis_index("modes")
    k = s // 4
    p = s % 4
    z = (p // 2) * 4 + m
    c = p % 2
    b = z * 2 + c

    def at_chip(col, zz, cc):
        return (col * 4 + (zz // 4) * 2 + cc, zz % 4)

    def at_block(col, bb):
        return at_chip(col, bb // 2, bb % 2)

    k_next, k_prev = (k + 1) % COLUMNS, (k + COLUMNS - 1) % COLUMNS
    b_next, b_prev = (b + 1) % 16, (b + 15) % 16
    hops = [(d, cc) for d in (4, 3, 5, 2, 6, 1, 7) for cc in (0, 1)]

    bar = pltpu.get_barrier_semaphore()

    def greet(dev):
        pl.semaphore_signal(bar, inc=1, device_id=dev, device_id_type=MESH)

    for d, cc in hops:
        greet(at_chip(k, (z + d) % 8, cc))
    greet(at_chip(k, z, 1 - c))
    greet(at_chip(k_next, z, c))
    greet(at_chip(k_prev, z, c))

    def remote(src, dst, ssem, rsem, dev):
        cp = pltpu.make_async_remote_copy(
            src, dst, ssem, rsem, device_id=dev, device_id_type=MESH
        )
        cp.start()

    def slot(ref, pp, mm):
        return ref.at[pp, pl.ds(pl.multiple_of(mm * SLOT, 8), SLOT)]

    def send_in(f, src, dst):
        for d, cc in hops:
            z2 = (z + d) % 8
            remote(src.at[z2 * 2 + cc], slot(dst, p, m), a_send.at[f], a_recv.at[f],
                   at_chip(k, z2, cc))
        remote(src.at[z * 2 + 1 - c], slot(dst, p, m), a_send.at[f], a_recv.at[f],
               at_chip(k, z, 1 - c))
        pltpu.make_async_copy(src.at[b], slot(dst, p, m), a_recv.at[f]).start()

    def send_out(f, src, dst):
        for d, cc in hops:
            z2 = (z + d) % 8
            remote(slot(src, (z2 // 4) * 2 + cc, z2 % 4), dst.at[b], a_send.at[f], a_recv.at[f],
                   at_chip(k, z2, cc))
        remote(slot(src, (z // 4) * 2 + 1 - c, m), dst.at[b], a_send.at[f], a_recv.at[f],
               at_chip(k, z, 1 - c))
        pltpu.make_async_copy(slot(src, p, m), dst.at[b], a_recv.at[f]).start()

    def await_all(f, buf):
        pltpu.make_async_copy(buf, buf, a_recv.at[f]).wait()

    def await_sent(f):
        part = sv.at[pl.ds(0, 15)]
        pltpu.make_async_copy(part, part, a_send.at[f]).wait()

    def halo(j, src, dst, dev):
        remote(src, dst, h_send.at[j], h_recv.at[j], dev)

    def await_halo(j, ref):
        pltpu.make_async_copy(ref, ref, h_recv.at[j]).wait()

    def await_halo_sent(j, ref):
        pltpu.make_async_copy(ref, ref, h_send.at[j]).wait()

    for bb in range(16):
        sv[bb, 0:GRP] = v_ref[pl.ds(bb, GRP, stride=16), :]
        sv[bb, GRP:SLOT] = avg_ref[bb : bb + 1, :]
    pl.semaphore_wait(bar, 17)
    send_in(0, sv, vc)
    for bb in range(16):
        gain = MIX / avg_ref[bb : bb + 1, :]
        su[bb, 0:GRP] = sv[bb, 0:GRP] + i_ref[pl.ds(bb, GRP, stride=16), :] * gain
        su[bb, GRP:SLOT] = zone_ref[bb : bb + 1, :].astype(F32)
    send_in(1, su, uc)
    for bb in range(16):
        st[bb, 0:GRP] = t_ref[pl.ds(bb, GRP, stride=16), :]
        st[bb, GRP:SLOT] = jnp.zeros((1, 128), F32)
    send_in(2, st, tc)

    def lanes(rows):
        return lax.broadcasted_iota(jnp.int32, (rows, 128), 1)

    tmp[...] = jnp.zeros((128, 512), F32)
    tmp[0:NPAR, 0:NMODE] = e_ref[...].astype(F32)
    raw = tmp[0:16, 0:256]
    lane = lax.broadcasted_iota(jnp.int32, (16, 256), 1)
    spaced = jnp.full((16, 256), FAR, F32)
    for g in range(4):
        here = (lane >= SLOT * g) & (lane < SLOT * g + GRP)
        spaced = jnp.where(here, raw if g == 0 else pltpu.roll(raw, g, 1), spaced)
    erow[...] = spaced
    tmp[0:16, 0:256] = spaced
    ecol[...] = jnp.transpose(tmp[:, 0:256])

    choice = n_ref[...]
    node = jnp.where(
        choice == 1, NODE_A,
        jnp.where(choice == 2, -NODE_A,
                  jnp.where(choice == 3, NODE_B, jnp.where(choice == 4, -NODE_B, 0.0))))
    tmp[...] = jnp.zeros((128, 512), F32)
    tmp[0:NPAR, :] = node
    hrow[0, 0:NPAR] = node
    hrow[1, 0:NPAR] = (node * node - 1.0) * (1.0 / math.sqrt(2.0))
    hrow[2, 0:NPAR] = (node * node * node - 3.0 * node) * (1.0 / math.sqrt(6.0))
    ncol[...] = jnp.transpose(tmp[...])

    def basis_rows(i, _):
        rows = pl.ds(pl.multiple_of(i * 8, 8), 8)
        acc = jnp.ones((8, NQ), F32)
        for par in range(NPAR):
            e = ecol[rows, par : par + 1]
            f = jnp.where(e == 1.0, hrow[0, par : par + 1, :], 1.0)
            f = jnp.where(e == 2.0, hrow[1, par : par + 1, :], f)
            f = jnp.where(e == 3.0, hrow[2, par : par + 1, :], f)
            acc = acc * f
        basis_t[rows, :] = jnp.where(ecol[rows, 0:1] < 50.0, acc, 0.0)
        return 0

    lax.fori_loop(0, KP // 8, basis_rows, 0)
    hi, lo = split(jnp.transpose(basis_t[...]))
    bcat[:, 0:KP] = hi
    bcat[:, KP : 2 * KP] = hi
    bcat[:, 2 * KP : 3 * KP] = lo
    weight = share_ref[...].astype(F32) * (1.0 / (512.0 * NQ * NMODE))
    hi, lo = split(basis_t[0:ROWS, :] * weight)
    wcat[:, 0:NQ] = hi
    wcat[:, NQ : 2 * NQ] = hi
    wcat[:, 2 * NQ : 3 * NQ] = lo

    def coupling_rows(i, _):
        rows = pl.ds(pl.multiple_of(i * 16, 16), 16)
        apart = jnp.zeros((16, KP), F32)
        acc = [jnp.zeros((16, KP), F32) for _ in range(NREG)]
        for par in range(NPAR):
            ei = ecol[rows, par : par + 1]
            ej = erow[par : par + 1, :]
            diff = jnp.abs(ei - ej)
            larger = jnp.maximum(ei, ej)
            root = jnp.where(larger == 1.0, 1.0,
                             jnp.where(larger == 2.0, math.sqrt(2.0), math.sqrt(3.0)))
            apart = apart + diff
            link = diff * root
            for r in range(NREG):
                acc[r] = acc[r] + zrr_ref[r, par] * link
        for r in range(NREG):
            hi, lo = split(jnp.where(apart == 1.0, acc[r], 0.0))
            out = pl.ds(pl.multiple_of(r * ROWS + i * 16, 16), 16)
            acat[out, 0:KP] = hi
            acat[out, KP : 2 * KP] = hi
            acat[out, 2 * KP : 3 * KP] = lo
        return 0

    lax.fori_loop(0, ROWS // 16, coupling_rows, 0)

    def lift_rows(i, _):
        rows = pl.ds(pl.multiple_of(i * 8, 8), 8)
        acc = [jnp.ones((8, 128), F32) for _ in range(NREG)]
        for par in range(NPAR):
            nd = jnp.broadcast_to(ncol[rows, par : par + 1], (8, 128))
            for r in range(NREG):
                acc[r] = acc[r] + zrr_ref[r, par] * nd
        for r in range(NREG):
            lift[r, rows, :] = acc[r]
        return 0

    lax.fori_loop(0, NQ // 8, lift_rows, 0)

    for part in range(3):
        gcat[part * KP + ROWS : (part + 1) * KP, :] = jnp.zeros((KP - ROWS, 3 * 512), BF16)
        rcat[part * KP + ROWS : (part + 1) * KP, :] = jnp.zeros((KP - ROWS, 512), BF16)

    lane1 = lanes(1)
    depth = lane1 % 8
    z_has_next = depth < 7
    z_has_prev = depth > 0
    low8 = lane1 < 8
    high8 = lane1 >= 120
    k_low = (k > 0).astype(F32)
    k_high = (k < COLUMNS - 1).astype(F32)
    b_low = (b > 0).astype(F32)
    b_high = (b < 15).astype(F32)

    def tfix_block(bb, _):
        cur = st[bb]
        before = st[jnp.maximum(bb - 1, 0)] * (bb > 0).astype(F32)
        after = st[jnp.minimum(bb + 1, 15)] * (bb < 15).astype(F32)
        y_next = jnp.where(high8, pltpu.roll(after, 120, 1), pltpu.roll(cur, 120, 1))
        y_prev = jnp.where(low8, pltpu.roll(before, 8, 1), pltpu.roll(cur, 8, 1))
        z_next = jnp.where(z_has_next, pltpu.roll(cur, 127, 1), 0.0)
        z_prev = jnp.where(z_has_prev, pltpu.roll(cur, 1, 1), 0.0)
        tfix[bb] = cur - 0.15 * (6.0 * cur - y_next - y_prev - z_next - z_prev)
        return 0

    lax.fori_loop(0, 16, tfix_block, 0)

    chunk = 32
    chunks = ROWS // chunk
    octet = lane1 // 8

    def chunk_of(i):
        return pl.ds(pl.multiple_of(i * chunk, chunk), chunk)

    def pack(src, dst):
        def body(i, _):
            rows = chunk_of(i)
            out = jnp.zeros((chunk, 128), F32)
            for q in range(4):
                x = src[q, rows, :]
                out = jnp.where(octet == q, pltpu.roll(x, 8 * q + 8, 1), out)
                out = jnp.where(octet == 4 + q, pltpu.roll(x, 32 + 8 * q, 1), out)
            dst[rows, :] = out
            return 0

        lax.fori_loop(0, chunks, body, 0)

    def y_pair(x, hy, q, rows):
        above = pltpu.roll(hy[1, rows, :] * b_high, 88 - 8 * q, 1)
        below = hy[0, rows, :] * b_low
        if q:
            below = pltpu.roll(below, 128 - 8 * q, 1)
        y_next = jnp.where(high8, above, pltpu.roll(x, 120, 1))
        y_prev = jnp.where(low8, below, pltpu.roll(x, 8, 1))
        return y_next, y_prev

    def z_pair(x):
        z_next = jnp.where(z_has_next, pltpu.roll(x, 127, 1), 0.0)
        z_prev = jnp.where(z_has_prev, pltpu.roll(x, 1, 1), 0.0)
        return z_next, z_prev

    def x_pair(field, hx, q, rows):
        x_next = field[q + 1, rows, :] if q < 3 else hx[1, rows, :] * k_high
        x_prev = field[q - 1, rows, :] if q > 0 else hx[0, rows, :] * k_low
        return x_next, x_prev

    def exchange_x(j, field, hx):
        halo(j, field.at[3], hx.at[0], at_chip(k_next, z, c))
        halo(j + 1, field.at[0], hx.at[1], at_chip(k_prev, z, c))

    def exchange_y(j, pk, hy):
        halo(j, pk, hy.at[0], at_block(k, b_next))
        halo(j + 1, pk, hy.at[1], at_block(k, b_prev))

    await_all(0, vc)
    exchange_x(0, vc, hxv)
    pack(vc, pkv)
    exchange_y(2, pkv, hyv)
    await_halo(0, hxv.at[0])
    await_halo(1, hxv.at[1])
    await_halo(2, hyv.at[0])
    await_halo(3, hyv.at[1])

    def rough_rows(i, _):
        rows = chunk_of(i)
        for q in range(4):
            x = vc[q, rows, :]
            y_next, y_prev = y_pair(x, hyv, q, rows)
            z_next, z_prev = z_pair(x)
            x_next, x_prev = x_pair(vc, hxv, q, rows)
            value = 6.0 * x - x_next - x_prev - z_next - z_prev - y_next - y_prev
            rough[q, rows, :] = value
            hi, lo = split(value)
            base = i * chunk
            cols = slice(128 * q, 128 * q + 128)
            rcat[pl.ds(pl.multiple_of(base, chunk), chunk), cols] = hi
            rcat[pl.ds(pl.multiple_of(base + KP, chunk), chunk), cols] = lo
            rcat[pl.ds(pl.multiple_of(base + 2 * KP, chunk), chunk), cols] = hi
        return 0

    lax.fori_loop(0, chunks, rough_rows, 0)

    def mix_region(r, _):
        rows = pl.ds(pl.multiple_of(r * ROWS, 32), ROWS)
        pmix[rows, :] = jnp.dot(acat[rows, :], rcat[...], preferred_element_type=F32)
        return 0

    lax.fori_loop(0, NREG, mix_region, 0)

    await_all(1, uc)
    zones = [uc[q, GRP : GRP + 1, :] for q in range(4)]
    avgs = [vc[q, GRP : GRP + 1, :] for q in range(4)]

    def relax_rows(i, _):
        rows = chunk_of(i)
        for q in range(4):
            cols = slice(128 * q, 128 * q + 128)
            part = [
                pmix[pl.ds(pl.multiple_of(r * ROWS + i * chunk, chunk), chunk), cols]
                for r in range(NREG)
            ]
            mixed = part[3]
            for r in range(3):
                mixed = jnp.where(zones[q] == float(r), part[r], mixed)
            rel[q, rows, :] = uc[q, rows, :] - MIX * (rough[q, rows, :] + mixed)
        return 0

    lax.fori_loop(0, chunks, relax_rows, 0)
    exchange_x(4, rel, hxr)
    pack(rel, pkr)
    exchange_y(6, pkr, hyr)
    send_out(3, rel, ro)

    def put_grad(i, col, value):
        hi, lo = split(value)
        base = i * chunk
        cols = slice(col, col + 128)
        gcat[pl.ds(pl.multiple_of(base, chunk), chunk), cols] = hi
        gcat[pl.ds(pl.multiple_of(base + KP, chunk), chunk), cols] = lo
        gcat[pl.ds(pl.multiple_of(base + 2 * KP, chunk), chunk), cols] = hi

    def grad_z(i, _):
        rows = chunk_of(i)
        for q in range(4):
            z_next, z_prev = z_pair(rel[q, rows, :])
            put_grad(i, 1024 + 128 * q, z_next - z_prev)
        return 0

    lax.fori_loop(0, chunks, grad_z, 0)

    def at_points(col, half):
        cols = pl.ds(pl.multiple_of(col + half * 256, 256), 256)
        return jnp.dot(bcat[...], gcat[:, cols], preferred_element_type=F32)

    def half_cols(half):
        return pl.ds(pl.multiple_of(half * 256, 256), 256)

    def points_z(half, _):
        g = at_points(1024, half)
        jsum[:, half_cols(half)] = g * g
        return 0

    lax.fori_loop(0, 2, points_z, 0)

    await_halo(4, hxr.at[0])
    await_halo(5, hxr.at[1])
    await_halo(6, hyr.at[0])
    await_halo(7, hyr.at[1])

    def grad_xy(i, _):
        rows = chunk_of(i)
        for q in range(4):
            y_next, y_prev = y_pair(rel[q, rows, :], hyr, q, rows)
            x_next, x_prev = x_pair(rel, hxr, q, rows)
            put_grad(i, 128 * q, x_next - x_prev)
            put_grad(i, 512 + 128 * q, y_next - y_prev)
        return 0

    lax.fori_loop(0, chunks, grad_xy, 0)

    def points_xy(half, _):
        cols = half_cols(half)
        g = at_points(0, half)
        jsum[:, cols] = jsum[:, cols] + g * g
        g = at_points(512, half)
        jsum[:, cols] = jsum[:, cols] + g * g
        return 0

    lax.fori_loop(0, 2, points_xy, 0)

    await_all(2, tc)
    exchange_x(8, tc, hxt)

    def joule_rows(i, _):
        rows = chunk_of(i)
        for q in range(4):
            gain = lift[3, rows, :]
            for r in range(3):
                gain = jnp.where(zones[q] == float(r), lift[r, rows, :], gain)
            cols = slice(128 * q, 128 * q + 128)
            hi, lo = split(jsum[rows, cols] * gain)
            base = i * chunk
            jcat[pl.ds(pl.multiple_of(base, chunk), chunk), cols] = hi
            jcat[pl.ds(pl.multiple_of(base + NQ, chunk), chunk), cols] = lo
            jcat[pl.ds(pl.multiple_of(base + 2 * NQ, chunk), chunk), cols] = hi
        return 0

    lax.fori_loop(0, NQ // chunk, joule_rows, 0)

    def heat_half(half, _):
        cols = half_cols(half)
        pmix[0:ROWS, cols] = jnp.dot(wcat[...], jcat[:, cols], preferred_element_type=F32)
        return 0

    lax.fori_loop(0, 2, heat_half, 0)
    await_halo(8, hxt.at[0])
    await_halo(9, hxt.at[1])

    def adv_rows(i, _):
        rows = chunk_of(i)
        for q in range(4):
            t_next, t_prev = x_pair(tc, hxt, q, rows)
            scale = avgs[q] * 0.025
            adv[q, rows, :] = (
                pmix[rows, 128 * q : 128 * q + 128] * scale + 0.15 * (t_next + t_prev)
            )
        return 0

    lax.fori_loop(0, chunks, adv_rows, 0)
    send_out(4, adv, ao)

    await_all(3, ro)
    for bb in range(16):
        rel_out[pl.ds(bb, GRP, stride=16), :] = ro[bb, 0:GRP]
    await_all(4, ao)
    for bb in range(16):
        adv_out[pl.ds(bb, GRP, stride=16), :] = ao[bb, 0:GRP] + tfix[bb, 0:GRP]
    for f in range(5):
        await_sent(f)
    for j in range(10):
        await_halo_sent(j, pkv)


def on_device(v, i, t, avg, zone, zrr, exps, choice, share):
    flat = lambda x: x.reshape(GRP * 16, 128)
    vmem = pl.BlockSpec(memory_space=pltpu.VMEM)
    smem = pl.BlockSpec(memory_space=pltpu.SMEM)
    field = pltpu.VMEM((4, ROWS, 128), F32)
    blocks = pltpu.VMEM((16, SLOT, 128), F32)
    pair = pltpu.VMEM((2, ROWS, 128), F32)
    one = pltpu.VMEM((ROWS, 128), F32)
    rel, adv = pl.pallas_call(
        kernel,
        out_shape=[jax.ShapeDtypeStruct((GRP * 16, 128), F32)] * 2,
        in_specs=[vmem] * 5 + [smem] + [vmem] * 3,
        out_specs=[vmem] * 2,
        scratch_shapes=[
            blocks, blocks, blocks, blocks,
            field, field, field, field, field, field,
            pair, pair, pair, pair, pair,
            one, one,
            blocks, blocks,
            pltpu.VMEM((128, 512), F32),
            pltpu.VMEM((256, 128), F32),
            pltpu.VMEM((16, 256), F32),
            pltpu.VMEM((3, 16, NQ), F32),
            pltpu.VMEM((NQ, 128), F32),
            pltpu.VMEM((KP, NQ), F32),
            pltpu.VMEM((NREG * ROWS, 3 * KP), BF16),
            pltpu.VMEM((NQ, 3 * KP), BF16),
            pltpu.VMEM((ROWS, 3 * NQ), BF16),
            pltpu.VMEM((3 * KP, 512), BF16),
            pltpu.VMEM((NREG * ROWS, 512), F32),
            pltpu.VMEM((3 * KP, 3 * 512), BF16),
            pltpu.VMEM((NQ, 512), F32),
            pltpu.VMEM((3 * NQ, 512), BF16),
            pltpu.VMEM((NREG, NQ, 128), F32),
            pltpu.SemaphoreType.DMA((5,)),
            pltpu.SemaphoreType.DMA((5,)),
            pltpu.SemaphoreType.DMA((10,)),
            pltpu.SemaphoreType.DMA((10,)),
        ],
        compiler_params=pltpu.CompilerParams(
            collective_id=0, has_side_effects=True, vmem_limit_bytes=60 << 20
        ),
        name="step",
    )(
        flat(v), flat(i), flat(t), avg.reshape(16, 128), zone.reshape(16, 128), zrr,
        exps.T, choice.T, share.reshape(1, NQ),
    )
    shape = (GRP, 1, 2048)
    return rel.reshape(shape), adv.reshape(shape)


def solution(mesh):
    field = P("modes", "space", None)
    cells = P("space", None)
    return jax.shard_map(
        on_device,
        mesh=mesh,
        in_specs=(field, field, field, cells, cells, P(), P(), P(), P()),
        out_specs=(field, field),
        check_vma=False,
    )
```

time: 266 us -> 82 us (0.31)
  the two profiles are of different devices: /device:TPU:61 before, /device:TPU:1 now
where the time goes in v1:
time: 82 us; the launch traced here: 81.8 us
  Pallas kernels  78.5 us (96%)
  local copies, waits for them, and re-layouts  2.63 us (3%)
    pallas_call x1, Pallas kernels, on_device(): pl.pallas_call(kernel, out_shape=[jax.ShapeDtypeStruct((GRP * 16, 128), F...  78.5 us
    unnamed x4, local copies, waits for them, and re-layouts  2.63 us

profile of v1, /device:TPU:1, one launch (start us, length us, event | category | flops | bytes accessed | tf_op | source)
XLA Modules:
  0.0 81.8 jit_solution(9218372773950516607)
XLA Ops:
  0.6 78.5 %step.1 = (f32[880,128]{1,0:T(8,128)}, f32[880,128]{1,0:T(8,128)}) custom-call(f32[880,128]{1,0:T(8,128)} %bitcast.10, f32[880,128]{1,0:T(8,128)} %bitcast.11, f32[880,128]{1,0:T(8,128)} %bitcast.12, f32[16,128]{1,0:T(8,128)} %bitcast.17, s32[16,128]{1,0:T(8,128)} %bitcast.18, f32[4,9]{1,0:T(4,128)} %zrr_ref.1, s32[9,220]{1,0:T(8,128)} %bitcast.16, ...), custom_call_target="tpu_custom_call" | custom-call | tf_op jit(solution)/shard_map/step/pallas_call | solution.py:468
  79.2 0.0 copy-start
  79.2 1.9 %copy.17 = f32[55,1,2048]{2,1,0:T(1,128)} copy(f32[55,1,2048]{2,1,0:T(1,128)} %bitcast.14) | data formatting | bytes 901120
  81.0 0.0 copy-done
  81.0 0.8 copy.18
Async XLA Ops:
  79.2 1.9 %copy-start = (f32[880,128]{1,0:T(8,128)S(1)}, f32[880,128]{1,0:T(8,128)}, u32[]{:S(2)}) copy-start(f32[880,128]{1,0:T(8,128)} %get-tuple-element.5) | copy-start | bytes 1351684

commit v2 on v1

v2 whole, which is shorter than its diff:
```python
import functools
import math

import jax
import jax.numpy as jnp
from jax import lax
from jax.experimental import pallas as pl
from jax.experimental.pallas import tpu as pltpu
from jax.sharding import PartitionSpec as P

MESH = pl.DeviceIdType.MESH
F32 = jnp.float32
BF16 = jnp.bfloat16
NODE_A = 1.355626179974266
NODE_B = 2.8569700138728056
NMODE = 220
NPAR = 9
NQ = 512
NREG = 4
GRP = 55
SLOT = 56
ROWS = 4 * SLOT
KP = 256
MIX = 0.8 / 6.0
COLUMNS = 32
FAR = 100.0


def split(x):
    hi = x.astype(BF16)
    return hi, (x - hi.astype(F32)).astype(BF16)


def kernel(
    v_hbm, i_hbm, t_hbm, avg_hbm, zone_hbm, zrr_ref, e_hbm, n_hbm, share_hbm,
    ro, ao, tfix_out,
    v_ref, i_ref, t_ref, avg_ref, zone_ref, e_ref, n_ref, share_ref,
    sv, su, st, tfix, vc, uc, tc, rel, adv, rough, hxv, hxr, hyr, hxt, sh, yh, pkr,
    tmp, ecol, erow, hrow, ncol, basis_t, acat, bcat, wcat, rcat, pmix, gcat, jsum, jcat, lift,
    in_sem, a_send, a_recv, h_send, h_recv,
):
    s = lax.axis_index("space")
    m = lax.axis_index("modes")
    k = s // 4
    p = s % 4
    z = (p // 2) * 4 + m
    c = p % 2
    b = z * 2 + c

    def at_chip(col, zz, cc):
        return (col * 4 + (zz // 4) * 2 + cc, zz % 4)

    def at_block(col, bb):
        return at_chip(col, bb // 2, bb % 2)

    k_next, k_prev = (k + 1) % COLUMNS, (k + COLUMNS - 1) % COLUMNS
    b_next, b_prev = (b + 1) % 16, (b + 15) % 16
    hops = [(d, cc) for d in (4, 3, 5, 2, 6, 1, 7) for cc in (0, 1)]

    loads = [
        pltpu.make_async_copy(src, dst, in_sem.at[n])
        for n, (src, dst) in enumerate((
            (v_hbm, v_ref), (avg_hbm, avg_ref), (i_hbm, i_ref), (zone_hbm, zone_ref),
            (t_hbm, t_ref), (e_hbm, e_ref), (n_hbm, n_ref), (share_hbm, share_ref)))
    ]
    loads[0].start()
    loads[1].start()

    bar = pltpu.get_barrier_semaphore()

    def greet(dev):
        pl.semaphore_signal(bar, inc=1, device_id=dev, device_id_type=MESH)

    for d, cc in hops:
        greet(at_chip(k, (z + d) % 8, cc))
    greet(at_chip(k, z, 1 - c))
    greet(at_chip(k_next, z, c))
    greet(at_chip(k_prev, z, c))
    for load in loads[2:]:
        load.start()

    def remote(src, dst, ssem, rsem, dev):
        cp = pltpu.make_async_remote_copy(
            src, dst, ssem, rsem, device_id=dev, device_id_type=MESH
        )
        cp.start()

    def slot(ref, pp, mm):
        return ref.at[pp, pl.ds(pl.multiple_of(mm * SLOT, 8), SLOT)]

    early = [hop for hop in hops if hop[0] in (3, 5)]
    late = [hop for hop in hops if hop[0] not in (3, 5)]

    def send_to(f, src, place, some):
        for d, cc in some:
            z2 = (z + d) % 8
            remote(src.at[z2 * 2 + cc], place, a_send.at[f], a_recv.at[f], at_chip(k, z2, cc))

    def send_rest(f, src, place):
        remote(src.at[z * 2 + 1 - c], place, a_send.at[f], a_recv.at[f], at_chip(k, z, 1 - c))
        pltpu.make_async_copy(src.at[b], place, a_recv.at[f]).start()

    def send_out(f, src, dst):
        for d, cc in hops:
            z2 = (z + d) % 8
            remote(slot(src, (z2 // 4) * 2 + cc, z2 % 4), dst.at[b], a_send.at[f], a_recv.at[f],
                   at_chip(k, z2, cc))
        remote(slot(src, (z // 4) * 2 + 1 - c, m), dst.at[b], a_send.at[f], a_recv.at[f],
               at_chip(k, z, 1 - c))
        pltpu.make_async_copy(slot(src, p, m), dst.at[b], a_recv.at[f]).start()

    def await_all(f, buf):
        pltpu.make_async_copy(buf, buf, a_recv.at[f]).wait()

    def await_sent(f, buf):
        part = buf.at[pl.ds(0, 15)]
        pltpu.make_async_copy(part, part, a_send.at[f]).wait()

    def halo(j, src, dst, dev):
        remote(src, dst, h_send.at[j], h_recv.at[j], dev)

    def await_halo(j, ref):
        pltpu.make_async_copy(ref, ref, h_recv.at[j]).wait()

    def await_halo_sent(j, ref):
        pltpu.make_async_copy(ref, ref, h_send.at[j]).wait()

    lane1 = lax.broadcasted_iota(jnp.int32, (1, 128), 1)
    low8 = lane1 < 8
    high8 = lane1 >= 120
    octet = lane1 // 8
    pair16 = lane1 // 16

    loads[0].wait()
    loads[1].wait()
    for bb in range(16):
        sv[bb, 0:GRP] = v_ref[pl.ds(bb, GRP, stride=16), :]
        sv[bb, GRP:SLOT] = avg_ref[bb : bb + 1, :]
    pl.semaphore_wait(bar, 17)
    send_to(0, sv, slot(vc, p, m), hops)
    send_rest(0, sv, slot(vc, p, m))

    def pack_edges(bb, _):
        before = sv[jnp.maximum(bb - 1, 0)] * (bb > 0).astype(F32)
        after = sv[jnp.minimum(bb + 1, 15)] * (bb < 15).astype(F32)
        both = jnp.where(high8, before, after)
        out = jnp.zeros((8, 128), F32)
        for t in range(7):
            moved = pltpu.roll(both[8 * t : 8 * t + 8], (16 * t + 8) % 128, 1)
            out = jnp.where(pair16 == t, moved, out)
        sh[bb] = out
        return 0

    lax.fori_loop(0, 16, pack_edges, 0)
    edge = yh.at[p, pl.ds(pl.multiple_of(m * 8, 8), 8)]
    send_to(5, sh, edge, hops)
    send_rest(5, sh, edge)
    loads[2].wait()
    loads[3].wait()
    for bb in range(16):
        gain = MIX / avg_ref[bb : bb + 1, :]
        su[bb, 0:GRP] = sv[bb, 0:GRP] + i_ref[pl.ds(bb, GRP, stride=16), :] * gain
        su[bb, GRP:SLOT] = zone_ref[bb : bb + 1, :].astype(F32)
    send_to(1, su, slot(uc, p, m), hops)
    send_rest(1, su, slot(uc, p, m))
    loads[4].wait()
    for bb in range(16):
        st[bb, 0:GRP] = t_ref[pl.ds(bb, GRP, stride=16), :]
        st[bb, GRP:SLOT] = jnp.zeros((1, 128), F32)
    send_to(2, st, slot(tc, p, m), early)
    for load in loads[5:]:
        load.wait()

    tmp[...] = jnp.zeros((128, 512), F32)
    tmp[0:NPAR, 0:NMODE] = e_ref[...].astype(F32)
    raw = tmp[0:16, 0:256]
    lane = lax.broadcasted_iota(jnp.int32, (16, 256), 1)
    spaced = jnp.full((16, 256), FAR, F32)
    for g in range(4):
        here = (lane >= SLOT * g) & (lane < SLOT * g + GRP)
        spaced = jnp.where(here, raw if g == 0 else pltpu.roll(raw, g, 1), spaced)
    erow[...] = spaced
    tmp[0:16, 0:256] = spaced
    ecol[...] = jnp.transpose(tmp[:, 0:256])

    choice = n_ref[...]
    node = jnp.where(
        choice == 1, NODE_A,
        jnp.where(choice == 2, -NODE_A,
                  jnp.where(choice == 3, NODE_B, jnp.where(choice == 4, -NODE_B, 0.0))))
    tmp[...] = jnp.zeros((128, 512), F32)
    tmp[0:NPAR, :] = node
    hrow[0, 0:NPAR] = node
    hrow[1, 0:NPAR] = (node * node - 1.0) * (1.0 / math.sqrt(2.0))
    hrow[2, 0:NPAR] = (node * node * node - 3.0 * node) * (1.0 / math.sqrt(6.0))
    ncol[...] = jnp.transpose(tmp[...])

    def basis_rows(i, _):
        rows = pl.ds(pl.multiple_of(i * 8, 8), 8)
        acc = jnp.ones((8, NQ), F32)
        for par in range(NPAR):
            e = ecol[rows, par : par + 1]
            f = jnp.where(e == 1.0, hrow[0, par : par + 1, :], 1.0)
            f = jnp.where(e == 2.0, hrow[1, par : par + 1, :], f)
            f = jnp.where(e == 3.0, hrow[2, par : par + 1, :], f)
            acc = acc * f
        basis_t[rows, :] = jnp.where(ecol[rows, 0:1] < 50.0, acc, 0.0)
        return 0

    lax.fori_loop(0, KP // 8, basis_rows, 0)
    hi, lo = split(jnp.transpose(basis_t[...]))
    bcat[:, 0:KP] = hi
    bcat[:, KP : 2 * KP] = hi
    bcat[:, 2 * KP : 3 * KP] = lo
    weight = share_ref[...].astype(F32) * (1.0 / (512.0 * NQ * NMODE))
    hi, lo = split(basis_t[0:ROWS, :] * weight)
    wcat[:, 0:NQ] = hi
    wcat[:, NQ : 2 * NQ] = hi
    wcat[:, 2 * NQ : 3 * NQ] = lo

    def coupling_rows(i, _):
        rows = pl.ds(pl.multiple_of(i * 16, 16), 16)
        apart = jnp.zeros((16, KP), F32)
        acc = [jnp.zeros((16, KP), F32) for _ in range(NREG)]
        for par in range(NPAR):
            ei = ecol[rows, par : par + 1]
            ej = erow[par : par + 1, :]
            diff = jnp.abs(ei - ej)
            larger = jnp.maximum(ei, ej)
            root = jnp.where(larger == 1.0, 1.0,
                             jnp.where(larger == 2.0, math.sqrt(2.0), math.sqrt(3.0)))
            apart = apart + diff
            link = diff * root
            for r in range(NREG):
                acc[r] = acc[r] + zrr_ref[r, par] * link
        for r in range(NREG):
            hi, lo = split(jnp.where(apart == 1.0, acc[r], 0.0))
            out = pl.ds(pl.multiple_of(r * ROWS + i * 16, 16), 16)
            acat[out, 0:KP] = hi
            acat[out, KP : 2 * KP] = hi
            acat[out, 2 * KP : 3 * KP] = lo
        return 0

    lax.fori_loop(0, ROWS // 16, coupling_rows, 0)

    for part in range(3):
        gcat[part * KP + ROWS : (part + 1) * KP, :] = jnp.zeros((KP - ROWS, 3 * 512), BF16)
        rcat[part * KP + ROWS : (part + 1) * KP, :] = jnp.zeros((KP - ROWS, 512), BF16)

    depth = lane1 % 8
    z_has_next = depth < 7
    z_has_prev = depth > 0
    k_low = (k > 0).astype(F32)
    k_high = (k < COLUMNS - 1).astype(F32)
    b_low = (b > 0).astype(F32)
    b_high = (b < 15).astype(F32)

    chunk = 32
    chunks = ROWS // chunk

    def chunk_of(i):
        return pl.ds(pl.multiple_of(i * chunk, chunk), chunk)

    def y_pair(x, edges):
        y_next = pltpu.roll(jnp.where(low8, edges, x), 120, 1)
        y_prev = pltpu.roll(jnp.where(high8, edges, x), 8, 1)
        return y_next, y_prev

    def z_pair(x):
        z_next = jnp.where(z_has_next, pltpu.roll(x, 127, 1), 0.0)
        z_prev = jnp.where(z_has_prev, pltpu.roll(x, 1, 1), 0.0)
        return z_next, z_prev

    def x_pair(field, hx, q, rows):
        x_next = field[q + 1, rows, :] if q < 3 else hx[1, rows, :] * k_high
        x_prev = field[q - 1, rows, :] if q > 0 else hx[0, rows, :] * k_low
        return x_next, x_prev

    def exchange_x(j, field, hx):
        halo(j, field.at[3], hx.at[0], at_chip(k_next, z, c))
        halo(j + 1, field.at[0], hx.at[1], at_chip(k_prev, z, c))

    def exchange_y(j, pk, hy):
        halo(j, pk, hy.at[0], at_block(k, b_next))
        halo(j + 1, pk, hy.at[1], at_block(k, b_prev))

    await_all(0, vc)
    exchange_x(0, vc, hxv)
    def lift_rows(i, _):
        rows = pl.ds(pl.multiple_of(i * 8, 8), 8)
        acc = [jnp.ones((8, 128), F32) for _ in range(NREG)]
        for par in range(NPAR):
            nd = jnp.broadcast_to(ncol[rows, par : par + 1], (8, 128))
            for r in range(NREG):
                acc[r] = acc[r] + zrr_ref[r, par] * nd
        for r in range(NREG):
            lift[r, rows, :] = acc[r]
        return 0

    lax.fori_loop(0, NQ // 8, lift_rows, 0)

    await_all(5, yh)
    await_halo(0, hxv.at[0])
    await_halo(1, hxv.at[1])

    def rough_group(g, _):
        for q in range(4):
            edges = yh[q, pl.ds(pl.multiple_of(g * 8, 8), 8), :]
            for t in range(7):
                rows = pl.ds(pl.multiple_of(g * SLOT + 8 * t, 8), 8)
                x = vc[q, rows, :]
                y_next, y_prev = y_pair(x, pltpu.roll(edges, 120 - 16 * t, 1))
                z_next, z_prev = z_pair(x)
                x_next, x_prev = x_pair(vc, hxv, q, rows)
                rough[q, rows, :] = (
                    6.0 * x - x_next - x_prev - z_next - z_prev - y_next - y_prev
                )
        return 0

    lax.fori_loop(0, 4, rough_group, 0)

    def rough_rows(i, _):
        for q in range(4):
            hi, lo = split(rough[q, chunk_of(i), :])
            base = i * chunk
            cols = slice(128 * q, 128 * q + 128)
            rcat[pl.ds(pl.multiple_of(base, chunk), chunk), cols] = hi
            rcat[pl.ds(pl.multiple_of(base + KP, chunk), chunk), cols] = lo
            rcat[pl.ds(pl.multiple_of(base + 2 * KP, chunk), chunk), cols] = hi
        return 0

    lax.fori_loop(0, chunks, rough_rows, 0)

    def mix_region(r, _):
        rows = pl.ds(pl.multiple_of(r * ROWS, 32), ROWS)
        pmix[rows, :] = jnp.dot(acat[rows, :], rcat[...], preferred_element_type=F32)
        return 0

    lax.fori_loop(0, NREG, mix_region, 0)

    await_all(1, uc)
    zones = [uc[q, GRP : GRP + 1, :] for q in range(4)]
    avgs = [vc[q, GRP : GRP + 1, :] for q in range(4)]

    def relax_rows(i, _):
        rows = chunk_of(i)
        for q in range(4):
            cols = slice(128 * q, 128 * q + 128)
            part = [
                pmix[pl.ds(pl.multiple_of(r * ROWS + i * chunk, chunk), chunk), cols]
                for r in range(NREG)
            ]
            mixed = part[3]
            for r in range(3):
                mixed = jnp.where(zones[q] == float(r), part[r], mixed)
            rel[q, rows, :] = uc[q, rows, :] - MIX * (rough[q, rows, :] + mixed)
        return 0

    lax.fori_loop(0, chunks, relax_rows, 0)
    exchange_x(4, rel, hxr)

    def pack_rel(i, _):
        out = jnp.zeros((8, 128), F32)
        for j in range(2):
            rows = pl.ds(pl.multiple_of(i * 16 + 8 * j, 8), 8)
            for q in range(4):
                moved = pltpu.roll(rel[q, rows, :], (64 * j + 16 * q + 8) % 128, 1)
                out = jnp.where(pair16 == 4 * j + q, moved, out)
        pkr[pl.ds(pl.multiple_of(i * 8, 8), 8), :] = out
        return 0

    lax.fori_loop(0, ROWS // 16, pack_rel, 0)
    exchange_y(6, pkr, hyr)
    send_to(2, st, slot(tc, p, m), late)
    send_rest(2, st, slot(tc, p, m))
    send_out(3, rel, ro)

    def put_grad(i, col, value):
        hi, lo = split(value)
        base = i * chunk
        cols = slice(col, col + 128)
        gcat[pl.ds(pl.multiple_of(base, chunk), chunk), cols] = hi
        gcat[pl.ds(pl.multiple_of(base + KP, chunk), chunk), cols] = lo
        gcat[pl.ds(pl.multiple_of(base + 2 * KP, chunk), chunk), cols] = hi

    def grad_z(i, _):
        rows = chunk_of(i)
        for q in range(4):
            z_next, z_prev = z_pair(rel[q, rows, :])
            put_grad(i, 1024 + 128 * q, z_next - z_prev)
        return 0

    lax.fori_loop(0, chunks, grad_z, 0)

    def at_points(col, half):
        cols = pl.ds(pl.multiple_of(col + half * 256, 256), 256)
        return jnp.dot(bcat[...], gcat[:, cols], preferred_element_type=F32)

    def half_cols(half):
        return pl.ds(pl.multiple_of(half * 256, 256), 256)

    def points_z(half, _):
        g = at_points(1024, half)
        jsum[:, half_cols(half)] = g * g
        return 0

    lax.fori_loop(0, 2, points_z, 0)

    await_halo(4, hxr.at[0])
    await_halo(5, hxr.at[1])
    await_halo(6, hyr.at[0])
    await_halo(7, hyr.at[1])

    def grad_xy(i, _):
        rows = chunk_of(i)
        packed = []
        for j in range(2):
            tile = pl.ds(pl.multiple_of(i * 16 + 8 * j, 8), 8)
            packed.append(
                jnp.where(octet % 2 == 0, hyr[0, tile, :] * b_low, hyr[1, tile, :] * b_high)
            )
        for q in range(4):
            edges = jnp.concatenate(
                [pltpu.roll(packed[j // 2], (120 - 64 * (j % 2) - 16 * q) % 128, 1)
                 for j in range(4)], axis=0)
            y_next, y_prev = y_pair(rel[q, rows, :], edges)
            x_next, x_prev = x_pair(rel, hxr, q, rows)
            put_grad(i, 128 * q, x_next - x_prev)
            put_grad(i, 512 + 128 * q, y_next - y_prev)
        return 0

    lax.fori_loop(0, chunks, grad_xy, 0)

    def points_xy(half, _):
        cols = half_cols(half)
        g = at_points(0, half)
        jsum[:, cols] = jsum[:, cols] + g * g
        g = at_points(512, half)
        jsum[:, cols] = jsum[:, cols] + g * g
        return 0

    lax.fori_loop(0, 2, points_xy, 0)

    await_all(2, tc)
    exchange_x(8, tc, hxt)

    def joule_rows(i, _):
        rows = chunk_of(i)
        for q in range(4):
            gain = lift[3, rows, :]
            for r in range(3):
                gain = jnp.where(zones[q] == float(r), lift[r, rows, :], gain)
            cols = slice(128 * q, 128 * q + 128)
            hi, lo = split(jsum[rows, cols] * gain)
            base = i * chunk
            jcat[pl.ds(pl.multiple_of(base, chunk), chunk), cols] = hi
            jcat[pl.ds(pl.multiple_of(base + NQ, chunk), chunk), cols] = lo
            jcat[pl.ds(pl.multiple_of(base + 2 * NQ, chunk), chunk), cols] = hi
        return 0

    lax.fori_loop(0, NQ // chunk, joule_rows, 0)

    def heat_half(half, _):
        cols = half_cols(half)
        pmix[0:ROWS, cols] = jnp.dot(wcat[...], jcat[:, cols], preferred_element_type=F32)
        return 0

    lax.fori_loop(0, 2, heat_half, 0)
    await_halo(8, hxt.at[0])
    await_halo(9, hxt.at[1])

    def adv_rows(i, _):
        rows = chunk_of(i)
        for q in range(4):
            t_next, t_prev = x_pair(tc, hxt, q, rows)
            scale = avgs[q] * 0.025
            adv[q, rows, :] = (
                pmix[rows, 128 * q : 128 * q + 128] * scale + 0.15 * (t_next + t_prev)
            )
        return 0

    lax.fori_loop(0, chunks, adv_rows, 0)
    send_out(4, adv, ao)

    def tfix_block(bb, _):
        cur = st[bb]
        before = st[jnp.maximum(bb - 1, 0)] * (bb > 0).astype(F32)
        after = st[jnp.minimum(bb + 1, 15)] * (bb < 15).astype(F32)
        y_next = jnp.where(high8, pltpu.roll(after, 120, 1), pltpu.roll(cur, 120, 1))
        y_prev = jnp.where(low8, pltpu.roll(before, 8, 1), pltpu.roll(cur, 8, 1))
        z_next = jnp.where(z_has_next, pltpu.roll(cur, 127, 1), 0.0)
        z_prev = jnp.where(z_has_prev, pltpu.roll(cur, 1, 1), 0.0)
        tfix[bb] = cur - 0.15 * (6.0 * cur - y_next - y_prev - z_next - z_prev)
        return 0

    lax.fori_loop(0, 16, tfix_block, 0)

    local = pltpu.make_async_copy(tfix, tfix_out, in_sem.at[0])
    local.start()
    await_all(3, ro)
    await_all(4, ao)
    local.wait()
    for f in range(5):
        await_sent(f, sv)
    await_sent(5, sh)
    for j in (0, 1, 4, 5, 8, 9):
        await_halo_sent(j, hxv.at[0])
    for j in (6, 7):
        await_halo_sent(j, pkr)


def assemble(ro, ao, tfix, rel_out, adv_out):
    for bb in range(16):
        rel_out[pl.ds(bb, GRP, stride=16), :] = ro[bb, 0:GRP]
        adv_out[pl.ds(bb, GRP, stride=16), :] = ao[bb, 0:GRP] + tfix[bb, 0:GRP]


def on_device(v, i, t, avg, zone, zrr, exps, choice, share):
    flat = lambda x: x.reshape(GRP * 16, 128)
    vmem = pl.BlockSpec(memory_space=pltpu.VMEM)
    hbm = pl.BlockSpec(memory_space=pl.ANY)
    smem = pl.BlockSpec(memory_space=pltpu.SMEM)
    field = pltpu.VMEM((4, ROWS, 128), F32)
    blocks = pltpu.VMEM((16, SLOT, 128), F32)
    pair = pltpu.VMEM((2, ROWS, 128), F32)
    flats = pltpu.VMEM((GRP * 16, 128), F32)
    packed = pltpu.VMEM((2, ROWS // 2, 128), F32)
    parts = pl.pallas_call(
        kernel,
        out_shape=[jax.ShapeDtypeStruct((16, SLOT, 128), F32)] * 3,
        in_specs=[hbm] * 5 + [smem] + [hbm] * 3,
        out_specs=[hbm] * 3,
        scratch_shapes=[
            flats, flats, flats,
            pltpu.VMEM((16, 128), F32),
            pltpu.VMEM((16, 128), jnp.int32),
            pltpu.VMEM((NPAR, NMODE), jnp.int32),
            pltpu.VMEM((NPAR, NQ), jnp.int32),
            pltpu.VMEM((1, NQ), jnp.int32),
            blocks, blocks, blocks, blocks,
            field, field, field, field, field, field,
            pair, pair, packed, pair,
            pltpu.VMEM((16, 8, 128), F32),
            pltpu.VMEM((4, 32, 128), F32),
            pltpu.VMEM((ROWS // 2, 128), F32),
            pltpu.VMEM((128, 512), F32),
            pltpu.VMEM((256, 128), F32),
            pltpu.VMEM((16, 256), F32),
            pltpu.VMEM((3, 16, NQ), F32),
            pltpu.VMEM((NQ, 128), F32),
            pltpu.VMEM((KP, NQ), F32),
            pltpu.VMEM((NREG * ROWS, 3 * KP), BF16),
            pltpu.VMEM((NQ, 3 * KP), BF16),
            pltpu.VMEM((ROWS, 3 * NQ), BF16),
            pltpu.VMEM((3 * KP, 512), BF16),
            pltpu.VMEM((NREG * ROWS, 512), F32),
            pltpu.VMEM((3 * KP, 3 * 512), BF16),
            pltpu.VMEM((NQ, 512), F32),
            pltpu.VMEM((3 * NQ, 512), BF16),
            pltpu.VMEM((NREG, NQ, 128), F32),
            pltpu.SemaphoreType.DMA((8,)),
            pltpu.SemaphoreType.DMA((6,)),
            pltpu.SemaphoreType.DMA((6,)),
            pltpu.SemaphoreType.DMA((10,)),
            pltpu.SemaphoreType.DMA((10,)),
        ],
        compiler_params=pltpu.CompilerParams(
            collective_id=0, has_side_effects=True, vmem_limit_bytes=60 << 20
        ),
        name="step",
    )(
        flat(v), flat(i), flat(t), avg.reshape(16, 128), zone.reshape(16, 128), zrr,
        exps.T, choice.T, share.reshape(1, NQ),
    )
    rel, adv = pl.pallas_call(
        assemble,
        out_shape=[jax.ShapeDtypeStruct((GRP * 16, 128), F32)] * 2,
        in_specs=[vmem] * 3,
        out_specs=[vmem] * 2,
        name="assemble",
    )(*parts)
    shape = (GRP, 1, 2048)
    return rel.reshape(shape), adv.reshape(shape)


def solution(mesh):
    field = P("modes", "space", None)
    cells = P("space", None)
    return jax.shard_map(
        on_device,
        mesh=mesh,
        in_specs=(field, field, field, cells, cells, P(), P(), P(), P()),
        out_specs=(field, field),
        check_vma=False,
    )
```

time: 82 us -> 73.2 us (0.89)
  Pallas kernels: 78.5 us -> 72.4 us
  local copies, waits for them, and re-layouts: 2.63 us -> 0 us
    pallas_call x1 -> x2, Pallas kernels: 78.5 us -> 72.4 us  [the longest x1 69.7 us: on_device(): pl.pallas_call(kernel, out_shape=[jax.ShapeDtypeStruct((16, SLOT, 128), F...]
    unnamed x4 -> x0, local copies, waits for them, and re-layouts: 2.63 us -> none
where the time goes in v2:
time: 73.2 us; the launch traced here: 73 us
  Pallas kernels  72.4 us (99%)
    pallas_call x1, Pallas kernels, on_device(): pl.pallas_call(kernel, out_shape=[jax.ShapeDtypeStruct((16, SLOT, 128), F...  69.7 us
    pallas_call x1, Pallas kernels, on_device(): pl.pallas_call(assemble, out_shape=[jax.ShapeDtypeStruct((GRP * 16, 128),...  2.64 us

profile of v2, /device:TPU:1, one launch (start us, length us, event | category | flops | bytes accessed | tf_op | source)
XLA Modules:
  0.0 73.0 jit_solution(5244332864129740143)
XLA Ops:
  0.6 69.7 %step.1 = (f32[16,56,128]{2,1,0:T(8,128)}, f32[16,56,128]{2,1,0:T(8,128)}, f32[16,56,128]{2,1,0:T(8,128)}) custom-call(f32[880,128]{1,0:T(8,128)} %bitcast.10, f32[880,128]{1,0:T(8,128)} %bitcast.11, f32[880,128]{1,0:T(8,128)} %bitcast.12, f32[16,128]{1,0:T(8,128)} %bitcast.15, s32[16,128]{1,0:T(8,128)} %bitcast.16, f32[4,9]{1,0:T(4,128)} %zrr_ref.1, ...), custom_call_target="tpu_custom_call" | custom-call | tf_op jit(solution)/shard_map/step/pallas_call | solution.py:528
  70.4 2.6 %assemble.1 = (f32[880,128]{1,0:T(8,128)}, f32[880,128]{1,0:T(8,128)}) custom-call(f32[16,56,128]{2,1,0:T(8,128)} %get-tuple-element.7.ro, f32[16,56,128]{2,1,0:T(8,128)} %get-tuple-element.8.ao, f32[16,56,128]{2,1,0:T(8,128)} %get-tuple-element.9.tfix), custom_call_target="tpu_custom_call" | custom-call | tf_op jit(solution)/shard_map/assemble/pallas_call | solution.py:575

commit v3 on v2

--- a/solution.py
+++ b/solution.py
@@ -32,10 +32,10 @@
 
 
 def kernel(
-    v_hbm, i_hbm, t_hbm, avg_hbm, zone_hbm, zrr_ref, e_hbm, n_hbm, share_hbm,
-    ro, ao, tfix_out,
-    v_ref, i_ref, t_ref, avg_ref, zone_ref, e_ref, n_ref, share_ref,
-    sv, su, st, tfix, vc, uc, tc, rel, adv, rough, hxv, hxr, hyr, hxt, sh, yh, pkr,
+    v_hbm, i_hbm, t_hbm, avg_hbm, zone_hbm, zrr_hbm, e_hbm, n_hbm, share_hbm,
+    rel_out, ao, tfix_out,
+    v_ref, i_ref, t_ref, avg_ref, zone_ref, zrr_ref, e_ref, n_ref, share_ref,
+    sv, su, st, tfix, vc, uc, tc, rel, adv, rough, ro, hxv, hyv, hxr, hyr, hxt, pkv, pkr,
     tmp, ecol, erow, hrow, ncol, basis_t, acat, bcat, wcat, rcat, pmix, gcat, jsum, jcat, lift,
     in_sem, a_send, a_recv, h_send, h_recv,
 ):
@@ -61,10 +61,13 @@
         pltpu.make_async_copy(src, dst, in_sem.at[n])
         for n, (src, dst) in enumerate((
             (v_hbm, v_ref), (avg_hbm, avg_ref), (i_hbm, i_ref), (zone_hbm, zone_ref),
-            (t_hbm, t_ref), (e_hbm, e_ref), (n_hbm, n_ref), (share_hbm, share_ref)))
+            (t_hbm, t_ref), (zrr_hbm, zrr_ref), (e_hbm, e_ref), (n_hbm, n_ref), (share_hbm, share_ref)))
     ]
     loads[0].start()
     loads[1].start()
+
+    for g in range(4):
+        tc[:, g * SLOT + GRP : (g + 1) * SLOT] = jnp.zeros((4, 1, 128), F32)
 
     bar = pltpu.get_barrier_semaphore()
 
@@ -85,35 +88,51 @@
         )
         cp.start()
 
-    def slot(ref, pp, mm):
-        return ref.at[pp, pl.ds(pl.multiple_of(mm * SLOT, 8), SLOT)]
-
-    early = [hop for hop in hops if hop[0] in (3, 5)]
-    late = [hop for hop in hops if hop[0] not in (3, 5)]
+    def slot(ref, pp, mm, size=SLOT):
+        return ref.at[pp, pl.ds(pl.multiple_of(mm * SLOT, 8), size)]
+
+    first = [hop for hop in hops if hop[0] in (3, 5)]
+    second = [hop for hop in hops if hop[0] in (4, 2, 6)]
+    third = [hop for hop in hops if hop[0] in (1, 7)]
 
     def send_to(f, src, place, some):
         for d, cc in some:
             z2 = (z + d) % 8
-            remote(src.at[z2 * 2 + cc], place, a_send.at[f], a_recv.at[f], at_chip(k, z2, cc))
+            remote(src.at[z2 * 2 + cc, pl.ds(0, place.shape[0])], place, a_send.at[f], a_recv.at[f], at_chip(k, z2, cc))
 
     def send_rest(f, src, place):
-        remote(src.at[z * 2 + 1 - c], place, a_send.at[f], a_recv.at[f], at_chip(k, z, 1 - c))
-        pltpu.make_async_copy(src.at[b], place, a_recv.at[f]).start()
-
-    def send_out(f, src, dst):
-        for d, cc in hops:
+        size = pl.ds(0, place.shape[0])
+        remote(src.at[z * 2 + 1 - c, size], place, a_send.at[f], a_recv.at[f],
+               at_chip(k, z, 1 - c))
+        pltpu.make_async_copy(src.at[b, size], place, a_recv.at[f]).start()
+
+    def send_out(f, src, dst, outer):
+        place = dst.at[b, pl.ds(0, GRP)]
+        for d in (4, 3, 5, 2, 6, 1, 7, 0):
             z2 = (z + d) % 8
-            remote(slot(src, (z2 // 4) * 2 + cc, z2 % 4), dst.at[b], a_send.at[f], a_recv.at[f],
-                   at_chip(k, z2, cc))
-        remote(slot(src, (z // 4) * 2 + 1 - c, m), dst.at[b], a_send.at[f], a_recv.at[f],
-               at_chip(k, z, 1 - c))
-        pltpu.make_async_copy(slot(src, p, m), dst.at[b], a_recv.at[f]).start()
+            zh = z2 // 4
+            cc = zh if outer else 1 - zh
+            if d:
+                remote(slot(src, zh * 2 + cc, z2 % 4, GRP), place, a_send.at[f], a_recv.at[f],
+                       at_chip(k, z2, cc))
+                continue
+            block = slot(src, zh * 2 + cc, m, GRP)
+
+            @pl.when(cc == c)
+            def _():
+                pltpu.make_async_copy(block, place, a_recv.at[f]).start()
+
+            @pl.when(cc != c)
+            def _():
+                remote(block, place, a_send.at[f], a_recv.at[f], at_chip(k, z, 1 - c))
 
     def await_all(f, buf):
+        if f >= 2:
+            buf = buf.at[:, pl.ds(0, 4 * GRP)] if f == 2 else buf.at[:, pl.ds(0, GRP)]
         pltpu.make_async_copy(buf, buf, a_recv.at[f]).wait()
 
     def await_sent(f, buf):
-        part = buf.at[pl.ds(0, 15)]
+        part = buf.at[pl.ds(0, 15), pl.ds(0, SLOT if f < 2 else GRP)]
         pltpu.make_async_copy(part, part, a_send.at[f]).wait()
 
     def halo(j, src, dst, dev):
@@ -140,34 +159,17 @@
     send_to(0, sv, slot(vc, p, m), hops)
     send_rest(0, sv, slot(vc, p, m))
 
-    def pack_edges(bb, _):
-        before = sv[jnp.maximum(bb - 1, 0)] * (bb > 0).astype(F32)
-        after = sv[jnp.minimum(bb + 1, 15)] * (bb < 15).astype(F32)
-        both = jnp.where(high8, before, after)
-        out = jnp.zeros((8, 128), F32)
-        for t in range(7):
-            moved = pltpu.roll(both[8 * t : 8 * t + 8], (16 * t + 8) % 128, 1)
-            out = jnp.where(pair16 == t, moved, out)
-        sh[bb] = out
-        return 0
-
-    lax.fori_loop(0, 16, pack_edges, 0)
-    edge = yh.at[p, pl.ds(pl.multiple_of(m * 8, 8), 8)]
-    send_to(5, sh, edge, hops)
-    send_rest(5, sh, edge)
+    loads[4].wait()
+    for bb in range(16):
+        st[bb, 0:GRP] = t_ref[pl.ds(bb, GRP, stride=16), :]
+        st[bb, GRP:SLOT] = jnp.zeros((1, 128), F32)
+    send_to(2, st, slot(tc, p, m, GRP), first)
     loads[2].wait()
     loads[3].wait()
     for bb in range(16):
         gain = MIX / avg_ref[bb : bb + 1, :]
         su[bb, 0:GRP] = sv[bb, 0:GRP] + i_ref[pl.ds(bb, GRP, stride=16), :] * gain
         su[bb, GRP:SLOT] = zone_ref[bb : bb + 1, :].astype(F32)
-    send_to(1, su, slot(uc, p, m), hops)
-    send_rest(1, su, slot(uc, p, m))
-    loads[4].wait()
-    for bb in range(16):
-        st[bb, 0:GRP] = t_ref[pl.ds(bb, GRP, stride=16), :]
-        st[bb, GRP:SLOT] = jnp.zeros((1, 128), F32)
-    send_to(2, st, slot(tc, p, m), early)
     for load in loads[5:]:
         load.wait()
 
@@ -286,6 +288,42 @@
 
     await_all(0, vc)
     exchange_x(0, vc, hxv)
+
+    def pack(src, dst):
+        def body(i, _):
+            for half in range(2):
+                out = jnp.zeros((8, 128), F32)
+                for j in range(2):
+                    rows = pl.ds(pl.multiple_of(i * 32 + 16 * half + 8 * j, 8), 8)
+                    for q in range(4):
+                        moved = pltpu.roll(src[q, rows, :], (64 * j + 16 * q + 8) % 128, 1)
+                        out = jnp.where(pair16 == 4 * j + q, moved, out)
+                dst[pl.ds(pl.multiple_of(i * 16 + 8 * half, 8), 8), :] = out
+            return 0
+
+        lax.fori_loop(0, ROWS // 32, body, 0, unroll=True)
+
+    def edges_of(hy, i):
+        both = []
+        for half in range(2):
+            tile = pl.ds(pl.multiple_of(i * 16 + 8 * half, 8), 8)
+            both.append(
+                jnp.where(octet % 2 == 0, hy[0, tile, :] * b_low, hy[1, tile, :] * b_high)
+            )
+        return [
+            jnp.concatenate(
+                [pltpu.roll(both[j // 2], (120 - 64 * (j % 2) - 16 * q) % 128, 1)
+                 for j in range(4)], axis=0)
+            for q in range(4)
+        ]
+
+    pack(vc, pkv)
+    exchange_y(2, pkv, hyv)
+    send_to(1, su, slot(uc, p, m), hops)
+    send_rest(1, su, slot(uc, p, m))
+    send_to(2, st, slot(tc, p, m, GRP), second)
+    send_rest(2, st, slot(tc, p, m, GRP))
+
     def lift_rows(i, _):
         rows = pl.ds(pl.multiple_of(i * 8, 8), 8)
         acc = [jnp.ones((8, 128), F32) for _ in range(NREG)]
@@ -299,29 +337,22 @@
 
     lax.fori_loop(0, NQ // 8, lift_rows, 0)
 
-    await_all(5, yh)
     await_halo(0, hxv.at[0])
     await_halo(1, hxv.at[1])
-
-    def rough_group(g, _):
+    await_halo(2, hyv.at[0])
+    await_halo(3, hyv.at[1])
+
+    def rough_rows(i, _):
+        rows = chunk_of(i)
+        edges = edges_of(hyv, i)
         for q in range(4):
-            edges = yh[q, pl.ds(pl.multiple_of(g * 8, 8), 8), :]
-            for t in range(7):
-                rows = pl.ds(pl.multiple_of(g * SLOT + 8 * t, 8), 8)
-                x = vc[q, rows, :]
-                y_next, y_prev = y_pair(x, pltpu.roll(edges, 120 - 16 * t, 1))
-                z_next, z_prev = z_pair(x)
-                x_next, x_prev = x_pair(vc, hxv, q, rows)
-                rough[q, rows, :] = (
-                    6.0 * x - x_next - x_prev - z_next - z_prev - y_next - y_prev
-                )
-        return 0
-
-    lax.fori_loop(0, 4, rough_group, 0)
-
-    def rough_rows(i, _):
-        for q in range(4):
-            hi, lo = split(rough[q, chunk_of(i), :])
+            x = vc[q, rows, :]
+            y_next, y_prev = y_pair(x, edges[q])
+            z_next, z_prev = z_pair(x)
+            x_next, x_prev = x_pair(vc, hxv, q, rows)
+            value = 6.0 * x - x_next - x_prev - z_next - z_prev - y_next - y_prev
+            rough[q, rows, :] = value
+            hi, lo = split(value)
             base = i * chunk
             cols = slice(128 * q, 128 * q + 128)
             rcat[pl.ds(pl.multiple_of(base, chunk), chunk), cols] = hi
@@ -358,22 +389,11 @@
 
     lax.fori_loop(0, chunks, relax_rows, 0)
     exchange_x(4, rel, hxr)
-
-    def pack_rel(i, _):
-        out = jnp.zeros((8, 128), F32)
-        for j in range(2):
-            rows = pl.ds(pl.multiple_of(i * 16 + 8 * j, 8), 8)
-            for q in range(4):
-                moved = pltpu.roll(rel[q, rows, :], (64 * j + 16 * q + 8) % 128, 1)
-                out = jnp.where(pair16 == 4 * j + q, moved, out)
-        pkr[pl.ds(pl.multiple_of(i * 8, 8), 8), :] = out
-        return 0
-
-    lax.fori_loop(0, ROWS // 16, pack_rel, 0)
+    pack(rel, pkr)
     exchange_y(6, pkr, hyr)
-    send_to(2, st, slot(tc, p, m), late)
-    send_rest(2, st, slot(tc, p, m))
-    send_out(3, rel, ro)
+    send_to(2, st, slot(tc, p, m, GRP), third)
+    send_out(3, rel, ro, False)
+    send_out(3, rel, ro, True)
 
     def put_grad(i, col, value):
         hi, lo = split(value)
@@ -413,17 +433,9 @@
 
     def grad_xy(i, _):
         rows = chunk_of(i)
-        packed = []
-        for j in range(2):
-            tile = pl.ds(pl.multiple_of(i * 16 + 8 * j, 8), 8)
-            packed.append(
-                jnp.where(octet % 2 == 0, hyr[0, tile, :] * b_low, hyr[1, tile, :] * b_high)
-            )
+        edges = edges_of(hyr, i)
         for q in range(4):
-            edges = jnp.concatenate(
-                [pltpu.roll(packed[j // 2], (120 - 64 * (j % 2) - 16 * q) % 128, 1)
-                 for j in range(4)], axis=0)
-            y_next, y_prev = y_pair(rel[q, rows, :], edges)
+            y_next, y_prev = y_pair(rel[q, rows, :], edges[q])
             x_next, x_prev = x_pair(rel, hxr, q, rows)
             put_grad(i, 128 * q, x_next - x_prev)
             put_grad(i, 512 + 128 * q, y_next - y_prev)
@@ -466,21 +478,25 @@
         return 0
 
     lax.fori_loop(0, 2, heat_half, 0)
+    def adv_rows(outer):
+        def body(i, _):
+            rows = chunk_of(i)
+            for q in (0, 3) if outer else (1, 2):
+                t_next, t_prev = x_pair(tc, hxt, q, rows)
+                scale = avgs[q] * 0.025
+                adv[q, rows, :] = (
+                    pmix[rows, 128 * q : 128 * q + 128] * scale + 0.15 * (t_next + t_prev)
+                )
+            return 0
+
+        lax.fori_loop(0, chunks, body, 0)
+
+    adv_rows(False)
+    send_out(4, adv, ao, False)
     await_halo(8, hxt.at[0])
     await_halo(9, hxt.at[1])
-
-    def adv_rows(i, _):
-        rows = chunk_of(i)
-        for q in range(4):
-            t_next, t_prev = x_pair(tc, hxt, q, rows)
-            scale = avgs[q] * 0.025
-            adv[q, rows, :] = (
-                pmix[rows, 128 * q : 128 * q + 128] * scale + 0.15 * (t_next + t_prev)
-            )
-        return 0
-
-    lax.fori_loop(0, chunks, adv_rows, 0)
-    send_out(4, adv, ao)
+    adv_rows(True)
+    send_out(4, adv, ao, True)
 
     def tfix_block(bb, _):
         cur = st[bb]
@@ -498,51 +514,61 @@
     local = pltpu.make_async_copy(tfix, tfix_out, in_sem.at[0])
     local.start()
     await_all(3, ro)
+    for bb in range(16):
+        v_ref[pl.ds(bb, GRP, stride=16), :] = ro[bb, 0:GRP]
+    final = pltpu.make_async_copy(v_ref, rel_out, in_sem.at[1])
+    final.start()
     await_all(4, ao)
     local.wait()
+    final.wait()
     for f in range(5):
         await_sent(f, sv)
-    await_sent(5, sh)
     for j in (0, 1, 4, 5, 8, 9):
         await_halo_sent(j, hxv.at[0])
-    for j in (6, 7):
+    for j in (2, 3, 6, 7):
         await_halo_sent(j, pkr)
 
 
-def assemble(ro, ao, tfix, rel_out, adv_out):
+def assemble(rel, ao, tfix, rel_out, adv_out, adv, sem):
+    first = pltpu.make_async_copy(rel, rel_out, sem.at[0])
+    first.start()
     for bb in range(16):
-        rel_out[pl.ds(bb, GRP, stride=16), :] = ro[bb, 0:GRP]
-        adv_out[pl.ds(bb, GRP, stride=16), :] = ao[bb, 0:GRP] + tfix[bb, 0:GRP]
+        adv[pl.ds(bb, GRP, stride=16), :] = ao[bb, 0:GRP] + tfix[bb, 0:GRP]
+    second = pltpu.make_async_copy(adv, adv_out, sem.at[1])
+    second.start()
+    first.wait()
+    second.wait()
 
 
 def on_device(v, i, t, avg, zone, zrr, exps, choice, share):
     flat = lambda x: x.reshape(GRP * 16, 128)
     vmem = pl.BlockSpec(memory_space=pltpu.VMEM)
-    hbm = pl.BlockSpec(memory_space=pl.ANY)
-    smem = pl.BlockSpec(memory_space=pltpu.SMEM)
+    hbm = pl.BlockSpec(memory_space=pltpu.HBM)
+    free = pl.BlockSpec(memory_space=pl.ANY)
     field = pltpu.VMEM((4, ROWS, 128), F32)
     blocks = pltpu.VMEM((16, SLOT, 128), F32)
     pair = pltpu.VMEM((2, ROWS, 128), F32)
     flats = pltpu.VMEM((GRP * 16, 128), F32)
+    edge = pltpu.VMEM((ROWS // 2, 128), F32)
     packed = pltpu.VMEM((2, ROWS // 2, 128), F32)
     parts = pl.pallas_call(
         kernel,
-        out_shape=[jax.ShapeDtypeStruct((16, SLOT, 128), F32)] * 3,
-        in_specs=[hbm] * 5 + [smem] + [hbm] * 3,
-        out_specs=[hbm] * 3,
+        out_shape=[jax.ShapeDtypeStruct((GRP * 16, 128), F32)]
+        + [jax.ShapeDtypeStruct((16, SLOT, 128), F32)] * 2,
+        in_specs=[hbm] * 9,
+        out_specs=[free] * 3,
         scratch_shapes=[
             flats, flats, flats,
             pltpu.VMEM((16, 128), F32),
             pltpu.VMEM((16, 128), jnp.int32),
+            pltpu.SMEM((NREG, NPAR), F32),
             pltpu.VMEM((NPAR, NMODE), jnp.int32),
             pltpu.VMEM((NPAR, NQ), jnp.int32),
             pltpu.VMEM((1, NQ), jnp.int32),
             blocks, blocks, blocks, blocks,
-            field, field, field, field, field, field,
-            pair, pair, packed, pair,
-            pltpu.VMEM((16, 8, 128), F32),
-            pltpu.VMEM((4, 32, 128), F32),
-            pltpu.VMEM((ROWS // 2, 128), F32),
+            field, field, field, field, field, field, blocks,
+            pair, packed, pair, packed, pair,
+            edge, edge,
             pltpu.VMEM((128, 512), F32),
             pltpu.VMEM((256, 128), F32),
             pltpu.VMEM((16, 256), F32),
@@ -558,25 +584,30 @@
             pltpu.VMEM((NQ, 512), F32),
             pltpu.VMEM((3 * NQ, 512), BF16),
             pltpu.VMEM((NREG, NQ, 128), F32),
-            pltpu.SemaphoreType.DMA((8,)),
-            pltpu.SemaphoreType.DMA((6,)),
-            pltpu.SemaphoreType.DMA((6,)),
+            pltpu.SemaphoreType.DMA((9,)),
+            pltpu.SemaphoreType.DMA((5,)),
+            pltpu.SemaphoreType.DMA((5,)),
             pltpu.SemaphoreType.DMA((10,)),
             pltpu.SemaphoreType.DMA((10,)),
         ],
         compiler_params=pltpu.CompilerParams(
-            collective_id=0, has_side_effects=True, vmem_limit_bytes=60 << 20
+            collective_id=0, has_side_effects=True, vmem_limit_bytes=36 << 20
         ),
         name="step",
-    )(
-        flat(v), flat(i), flat(t), avg.reshape(16, 128), zone.reshape(16, 128), zrr,
-        exps.T, choice.T, share.reshape(1, NQ),
-    )
+    )(*(
+        pltpu.with_memory_space_constraint(x, pltpu.HBM)
+        for x in (
+            flat(v), flat(i), flat(t), avg.reshape(16, 128), zone.reshape(16, 128), zrr,
+            exps.T, choice.T, share.reshape(1, NQ),
+        )
+    ))
     rel, adv = pl.pallas_call(
         assemble,
         out_shape=[jax.ShapeDtypeStruct((GRP * 16, 128), F32)] * 2,
-        in_specs=[vmem] * 3,
-        out_specs=[vmem] * 2,
+        in_specs=[free, vmem, vmem],
+        out_specs=[free] * 2,
+        scratch_shapes=[flats, pltpu.SemaphoreType.DMA((2,))],
+        compiler_params=pltpu.CompilerParams(vmem_limit_bytes=16 << 20),
         name="assemble",
     )(*parts)
     shape = (GRP, 1, 2048)

time: 73.2 us -> 66.8 us (0.913)
  Pallas kernels: 72.4 us -> 65.7 us
    pallas_call x1, Pallas kernels: 69.7 us -> 64.7 us  [on_device(): pl.pallas_call(kernel, out_shape=[jax.ShapeDtypeStruct((GRP * 16, 128), F...]
    pallas_call x1, Pallas kernels: 2.64 us -> 1.02 us  [on_device(): pl.pallas_call(assemble, out_shape=[jax.ShapeDtypeStruct((GRP * 16, 128),...]
where the time goes in v3:
time: 66.8 us; the launch traced here: 66.3 us
  Pallas kernels  65.7 us (98%)
    pallas_call x1, Pallas kernels, on_device(): pl.pallas_call(kernel, out_shape=[jax.ShapeDtypeStruct((GRP * 16, 128), F...  64.7 us

profile of v3, /device:TPU:1, one launch (start us, length us, event | category | flops | bytes accessed | tf_op | source)
XLA Modules:
  0.0 66.3 jit_solution(15727696895455588455)
XLA Ops:
  0.6 64.7 %step.1 = (f32[880,128]{1,0:T(8,128)S(1)}, f32[16,56,128]{2,1,0:T(8,128)S(1)}, f32[16,56,128]{2,1,0:T(8,128)S(1)}) custom-call(f32[880,128]{1,0:T(8,128)} %bitcast.10, f32[880,128]{1,0:T(8,128)} %bitcast.11, f32[880,128]{1,0:T(8,128)} %bitcast.12, f32[16,128]{1,0:T(8,128)} %bitcast.15, s32[16,128]{1,0:T(8,128)} %bitcast.16, f32[4,9]{1,0:T(4,128)} %zrr_hbm.1, ...), custom_call_target="tpu_custom_call" | custom-call | tf_op jit(solution)/shard_map/step/pallas_call | solution.py:554
  65.3 1.0 %assemble.1 = (f32[880,128]{1,0:T(8,128)}, f32[880,128]{1,0:T(8,128)}) custom-call(f32[880,128]{1,0:T(8,128)S(1)} %get-tuple-element.7.rel, f32[16,56,128]{2,1,0:T(8,128)S(1)} %get-tuple-element.8.ao, f32[16,56,128]{2,1,0:T(8,128)S(1)} %get-tuple-element.9.tfix), custom_call_target="tpu_custom_call" | custom-call | tf_op jit(solution)/shard_map/assemble/pallas_call | solution.py:604

commit v4 on v3

--- a/solution.py
+++ b/solution.py
@@ -148,7 +148,6 @@
     low8 = lane1 < 8
     high8 = lane1 >= 120
     octet = lane1 // 8
-    pair16 = lane1 // 16
 
     loads[0].wait()
     loads[1].wait()
@@ -264,8 +263,9 @@
         return pl.ds(pl.multiple_of(i * chunk, chunk), chunk)
 
     def y_pair(x, edges):
-        y_next = pltpu.roll(jnp.where(low8, edges, x), 120, 1)
-        y_prev = pltpu.roll(jnp.where(high8, edges, x), 8, 1)
+        after, before = edges
+        y_next = jnp.where(high8, after, pltpu.roll(x, 120, 1))
+        y_prev = jnp.where(low8, before, pltpu.roll(x, 8, 1))
         return y_next, y_prev
 
     def z_pair(x):
@@ -283,37 +283,35 @@
         halo(j + 1, field.at[0], hx.at[1], at_chip(k_prev, z, c))
 
     def exchange_y(j, pk, hy):
-        halo(j, pk, hy.at[0], at_block(k, b_next))
-        halo(j + 1, pk, hy.at[1], at_block(k, b_prev))
+        halo(j, pk.at[0], hy.at[0], at_block(k, b_next))
+        halo(j + 1, pk.at[1], hy.at[1], at_block(k, b_prev))
 
     await_all(0, vc)
     exchange_x(0, vc, hxv)
 
+    def turn(x, shift):
+        return pltpu.roll(x, shift % 128, 1) if shift % 128 else x
+
     def pack(src, dst):
-        def body(i, _):
-            for half in range(2):
-                out = jnp.zeros((8, 128), F32)
-                for j in range(2):
-                    rows = pl.ds(pl.multiple_of(i * 32 + 16 * half + 8 * j, 8), 8)
-                    for q in range(4):
-                        moved = pltpu.roll(src[q, rows, :], (64 * j + 16 * q + 8) % 128, 1)
-                        out = jnp.where(pair16 == 4 * j + q, moved, out)
-                dst[pl.ds(pl.multiple_of(i * 16 + 8 * half, 8), 8), :] = out
-            return 0
-
-        lax.fori_loop(0, ROWS // 32, body, 0, unroll=True)
+        for i in range(chunks):
+            last = jnp.zeros((8, 128), F32)
+            start = jnp.zeros((8, 128), F32)
+            for j in range(4):
+                for q in range(4):
+                    x = src[q, 32 * i + 8 * j : 32 * i + 8 * j + 8, :]
+                    here = octet == 4 * j + q
+                    last = jnp.where(here, turn(x, 32 * j + 8 * q + 8), last)
+                    start = jnp.where(here, turn(x, 32 * j + 8 * q), start)
+            dst[0, 8 * i : 8 * i + 8, :] = last
+            dst[1, 8 * i : 8 * i + 8, :] = start
 
     def edges_of(hy, i):
-        both = []
-        for half in range(2):
-            tile = pl.ds(pl.multiple_of(i * 16 + 8 * half, 8), 8)
-            both.append(
-                jnp.where(octet % 2 == 0, hy[0, tile, :] * b_low, hy[1, tile, :] * b_high)
-            )
+        tile = pl.ds(pl.multiple_of(i * 8, 8), 8)
+        below = hy[0, tile, :] * b_low
+        above = hy[1, tile, :] * b_high
         return [
-            jnp.concatenate(
-                [pltpu.roll(both[j // 2], (120 - 64 * (j % 2) - 16 * q) % 128, 1)
-                 for j in range(4)], axis=0)
+            (jnp.concatenate([turn(above, 120 - 32 * j - 8 * q) for j in range(4)], axis=0),
+             jnp.concatenate([turn(below, -32 * j - 8 * q) for j in range(4)], axis=0))
             for q in range(4)
         ]
 
@@ -518,15 +516,16 @@
         v_ref[pl.ds(bb, GRP, stride=16), :] = ro[bb, 0:GRP]
     final = pltpu.make_async_copy(v_ref, rel_out, in_sem.at[1])
     final.start()
-    await_all(4, ao)
-    local.wait()
-    final.wait()
-    for f in range(5):
+    for f in range(4):
         await_sent(f, sv)
     for j in (0, 1, 4, 5, 8, 9):
         await_halo_sent(j, hxv.at[0])
     for j in (2, 3, 6, 7):
-        await_halo_sent(j, pkr)
+        await_halo_sent(j, pkr.at[0])
+    local.wait()
+    final.wait()
+    await_sent(4, sv)
+    await_all(4, ao)
 
 
 def assemble(rel, ao, tfix, rel_out, adv_out, adv, sem):
@@ -549,8 +548,7 @@
     blocks = pltpu.VMEM((16, SLOT, 128), F32)
     pair = pltpu.VMEM((2, ROWS, 128), F32)
     flats = pltpu.VMEM((GRP * 16, 128), F32)
-    edge = pltpu.VMEM((ROWS // 2, 128), F32)
-    packed = pltpu.VMEM((2, ROWS // 2, 128), F32)
+    packed = pltpu.VMEM((2, ROWS // 4, 128), F32)
     parts = pl.pallas_call(
         kernel,
         out_shape=[jax.ShapeDtypeStruct((GRP * 16, 128), F32)]
@@ -568,7 +566,7 @@
             blocks, blocks, blocks, blocks,
             field, field, field, field, field, field, blocks,
             pair, packed, pair, packed, pair,
-            edge, edge,
+            packed, packed,
             pltpu.VMEM((128, 512), F32),
             pltpu.VMEM((256, 128), F32),
             pltpu.VMEM((16, 256), F32),

time: 66.8 us -> 66.1 us (0.990)
  Pallas kernels: 65.7 us -> 64.9 us
    pallas_call x1, Pallas kernels: 64.7 us -> 63.9 us  [on_device(): pl.pallas_call(kernel, out_shape=[jax.ShapeDtypeStruct((GRP * 16, 128), F...]
where the time goes in v4:
time: 66.1 us; the launch traced here: 65.5 us
  Pallas kernels  64.9 us (98%)
    pallas_call x1, Pallas kernels, on_device(): pl.pallas_call(kernel, out_shape=[jax.ShapeDtypeStruct((GRP * 16, 128), F...  63.9 us

profile of v4, /device:TPU:1, one launch (start us, length us, event | category | flops | bytes accessed | tf_op | source)
XLA Modules:
  0.0 65.5 jit_solution(17065187811439079614)
XLA Ops:
  0.6 63.9 %step.1 = (f32[880,128]{1,0:T(8,128)S(1)}, f32[16,56,128]{2,1,0:T(8,128)S(1)}, f32[16,56,128]{2,1,0:T(8,128)S(1)}) custom-call(f32[880,128]{1,0:T(8,128)} %bitcast.10, f32[880,128]{1,0:T(8,128)} %bitcast.11, f32[880,128]{1,0:T(8,128)} %bitcast.12, f32[16,128]{1,0:T(8,128)} %bitcast.15, s32[16,128]{1,0:T(8,128)} %bitcast.16, f32[4,9]{1,0:T(4,128)} %zrr_hbm.1, ...), custom_call_target="tpu_custom_call" | custom-call | tf_op jit(solution)/shard_map/step/pallas_call | solution.py:552
  64.5 1.0 %assemble.1 = (f32[880,128]{1,0:T(8,128)}, f32[880,128]{1,0:T(8,128)}) custom-call(f32[880,128]{1,0:T(8,128)S(1)} %get-tuple-element.7.rel, f32[16,56,128]{2,1,0:T(8,128)S(1)} %get-tuple-element.8.ao, f32[16,56,128]{2,1,0:T(8,128)S(1)} %get-tuple-element.9.tfix), custom_call_target="tpu_custom_call" | custom-call | tf_op jit(solution)/shard_map/assemble/pallas_call | solution.py:602

commit v5 on v4

--- a/solution.py
+++ b/solution.py
@@ -92,8 +92,9 @@
         return ref.at[pp, pl.ds(pl.multiple_of(mm * SLOT, 8), size)]
 
     first = [hop for hop in hops if hop[0] in (3, 5)]
-    second = [hop for hop in hops if hop[0] in (4, 2, 6)]
-    third = [hop for hop in hops if hop[0] in (1, 7)]
+    rest = [hop for hop in hops if hop[0] not in (3, 5)]
+    early = [hop for hop in hops if hop[0] in (3, 5, 1, 7)]
+    late = [hop for hop in hops if hop[0] in (4, 2, 6)]
 
     def send_to(f, src, place, some):
         for d, cc in some:
@@ -158,17 +159,17 @@
     send_to(0, sv, slot(vc, p, m), hops)
     send_rest(0, sv, slot(vc, p, m))
 
-    loads[4].wait()
-    for bb in range(16):
-        st[bb, 0:GRP] = t_ref[pl.ds(bb, GRP, stride=16), :]
-        st[bb, GRP:SLOT] = jnp.zeros((1, 128), F32)
-    send_to(2, st, slot(tc, p, m, GRP), first)
     loads[2].wait()
     loads[3].wait()
     for bb in range(16):
         gain = MIX / avg_ref[bb : bb + 1, :]
         su[bb, 0:GRP] = sv[bb, 0:GRP] + i_ref[pl.ds(bb, GRP, stride=16), :] * gain
         su[bb, GRP:SLOT] = zone_ref[bb : bb + 1, :].astype(F32)
+    send_to(1, su, slot(uc, p, m), first)
+    loads[4].wait()
+    for bb in range(16):
+        st[bb, 0:GRP] = t_ref[pl.ds(bb, GRP, stride=16), :]
+        st[bb, GRP:SLOT] = jnp.zeros((1, 128), F32)
     for load in loads[5:]:
         load.wait()
 
@@ -317,9 +318,9 @@
 
     pack(vc, pkv)
     exchange_y(2, pkv, hyv)
-    send_to(1, su, slot(uc, p, m), hops)
+    send_to(1, su, slot(uc, p, m), rest)
     send_rest(1, su, slot(uc, p, m))
-    send_to(2, st, slot(tc, p, m, GRP), second)
+    send_to(2, st, slot(tc, p, m, GRP), early)
     send_rest(2, st, slot(tc, p, m, GRP))
 
     def lift_rows(i, _):
@@ -389,7 +390,7 @@
     exchange_x(4, rel, hxr)
     pack(rel, pkr)
     exchange_y(6, pkr, hyr)
-    send_to(2, st, slot(tc, p, m, GRP), third)
+    send_to(2, st, slot(tc, p, m, GRP), late)
     send_out(3, rel, ro, False)
     send_out(3, rel, ro, True)
 

time: 66.1 us -> 65.8 us (level)
  no operation moved by 1% of the time
where the time goes in v5:
time: 65.8 us; the launch traced here: 65.5 us
  Pallas kernels  64.8 us (98%)
    pallas_call x1, Pallas kernels, on_device(): pl.pallas_call(kernel, out_shape=[jax.ShapeDtypeStruct((GRP * 16, 128), F...  63.8 us

profile of v5, /device:TPU:1, one launch (start us, length us, event | category | flops | bytes accessed | tf_op | source)
XLA Modules:
  0.0 65.5 jit_solution(4827182819826638725)
XLA Ops:
  0.6 63.8 %step.1 = (f32[880,128]{1,0:T(8,128)S(1)}, f32[16,56,128]{2,1,0:T(8,128)S(1)}, f32[16,56,128]{2,1,0:T(8,128)S(1)}) custom-call(f32[880,128]{1,0:T(8,128)} %bitcast.10, f32[880,128]{1,0:T(8,128)} %bitcast.11, f32[880,128]{1,0:T(8,128)} %bitcast.12, f32[16,128]{1,0:T(8,128)} %bitcast.15, s32[16,128]{1,0:T(8,128)} %bitcast.16, f32[4,9]{1,0:T(4,128)} %zrr_hbm.1, ...), custom_call_target="tpu_custom_call" | custom-call | tf_op jit(solution)/shard_map/step/pallas_call | solution.py:553
  64.4 1.0 %assemble.1 = (f32[880,128]{1,0:T(8,128)}, f32[880,128]{1,0:T(8,128)}) custom-call(f32[880,128]{1,0:T(8,128)S(1)} %get-tuple-element.7.rel, f32[16,56,128]{2,1,0:T(8,128)S(1)} %get-tuple-element.8.ao, f32[16,56,128]{2,1,0:T(8,128)S(1)} %get-tuple-element.9.tfix), custom_call_target="tpu_custom_call" | custom-call | tf_op jit(solution)/shard_map/assemble/pallas_call | solution.py:603
